TPU v7x, 32 devices: a whole 2x2x4 slice. The times are simulated.
32 devices in a mesh: parts: 2 (over y), tile: 4 (over z), depth: 2 (over x), sub: 2 (over core).
Axes of the slice: x: 2, y: 2, z: 4, core: 2. Of those that a mesh axis runs over, the one named last changes fastest.
Arguments:
- left_mantissa: bfloat16 [512, 512], P(('parts', 'depth'), 'tile'), parts along dimension 0, may hold values from -6 to 6
- left_exponent: int32 [512, 16], P(('parts', 'depth'), 'tile'), parts along dimension 0, may hold values from -2 to 1
- right_mantissa: bfloat16 [512, 512], P(('parts', 'depth'), ('tile', 'sub')), parts along dimension 0, may hold values from -6 to 6
- right_exponent: int32 [512, 16], P(('parts', 'depth'), ('tile', 'sub')), parts along dimension 0, may hold values from -2 to 1
- residue_mask: int32 [32], P('parts'), parts along dimension 0, may hold values 0 or 1
- out_weight: bfloat16 [1024, 128], replicated, may hold values from -3 to 3
- out_bias: float32 [128], replicated, may hold values from -3 to 3
- gate_weight: bfloat16 [128, 512], replicated, may hold values from -0.5 to 0.5
- up_weight: bfloat16 [128, 512], replicated, may hold values from -0.5 to 0.5
- down_weight: bfloat16 [512, 128], replicated, may hold values from -0.25 to 0.25
- distogram_weight: bfloat16 [128, 64], replicated, may hold values from -0.5 to 0.5
- distogram_bias: float32 [64], replicated, may hold values from -3 to 3
Outputs:
- symmetric_pair: bfloat16 [32, 2048], P(('parts', 'tile', 'depth', 'sub')), parts along dimension 0
- distogram: float32 [32, 1024], P(('parts', 'tile', 'depth', 'sub')), parts along dimension 0
There are 2 independent parts, one for each index of `parts`. A program takes and returns all parts, laid end to end along the dimension named above; an argument that names none is the same for every part. Nothing has to cross between parts.
All inputs are finite; a program needn't handle non-finite values.
Results may differ from a plain program's by a relative error of at most 0.007.
Values may be sent and summed in bfloat16 or wider, within the bound.
No kernel may reach another device: no remote copies, remote signals or barrier semaphores. Data moves between devices by JAX's collectives and lax.ppermute only.
A program may use at most 64 MiB of HBM per device.

v0:
```python
import jax
import jax.numpy as jnp
from jax import lax
from jax.sharding import PartitionSpec as P


def dequantize(mantissa, exponent, keep_mask):
    seq_count, columns = mantissa.shape
    residues = exponent.shape[1]
    channels = columns // residues
    scaling = (
        jnp.exp2(exponent.astype(jnp.float32))[:, :, None]
        * keep_mask.astype(jnp.float32)[None, :, None]
    )
    values = mantissa.astype(jnp.float32).reshape(seq_count, residues, channels) * scaling
    return values.astype(jnp.bfloat16).reshape(seq_count, columns)


def transition(pair_rows, gate_weight, up_weight, down_weight):
    values = pair_rows.astype(jnp.float32)
    center = jnp.mean(values, axis=-1, keepdims=True)
    spread = jnp.mean((values - center) ** 2, axis=-1, keepdims=True)
    normed = ((values - center) * lax.rsqrt(spread + 1e-05)).astype(jnp.bfloat16)
    gate_part = jnp.dot(normed, gate_weight, preferred_element_type=jnp.float32)
    up_part = jnp.dot(normed, up_weight, preferred_element_type=jnp.float32)
    hidden = (jax.nn.silu(gate_part) * up_part).astype(jnp.bfloat16)
    return (values + jnp.dot(hidden, down_weight, preferred_element_type=jnp.float32)).astype(
        jnp.bfloat16
    )


def outer_block(row_factor, col_factor, projector, group_rows):
    channels = projector.shape[0]
    row_count = row_factor.shape[1] // channels
    col_count = col_factor.shape[1] // channels
    block_count = row_count // group_rows

    def one_block(block_index):
        row_slice = lax.dynamic_slice_in_dim(
            row_factor, block_index * (group_rows * channels), group_rows * channels, 1
        )
        outer = lax.dot_general(
            row_slice, col_factor, (((0,), (0,)), ((), ())), preferred_element_type=jnp.float32
        )
        outer = outer.reshape(group_rows, channels, col_count, channels)
        return jnp.einsum("icje,cek->ijk", outer, projector, precision=lax.Precision.HIGHEST)

    blocks = lax.map(one_block, jnp.arange(block_count, dtype=jnp.int32))
    return blocks.reshape(row_count, col_count, projector.shape[2])


def per_device(
    left_mantissa,
    left_exponent,
    right_mantissa,
    right_exponent,
    residue_mask,
    out_weight,
    out_bias,
    gate_weight,
    up_weight,
    down_weight,
    distogram_weight,
    distogram_bias,
):
    tile_count = lax.axis_size("tile")
    depth_count = lax.axis_size("depth")
    sub_count = lax.axis_size("sub")
    seq_group = left_mantissa.shape[0]
    band_width = left_exponent.shape[1]
    channels = left_mantissa.shape[1] // band_width
    residues = residue_mask.shape[0]
    rows_here = band_width // (depth_count * sub_count)
    pair_channels = out_weight.shape[1]
    total_seqs = seq_group * depth_count
    band_keep = lax.dynamic_slice_in_dim(
        residue_mask, lax.axis_index("tile") * band_width, band_width
    )
    piece_width = right_exponent.shape[1]
    piece_keep = lax.dynamic_slice_in_dim(
        residue_mask,
        (lax.axis_index("tile") * sub_count + lax.axis_index("sub")) * piece_width,
        piece_width,
    )
    left_band = dequantize(left_mantissa, left_exponent, band_keep)
    left_band = left_band.reshape(seq_group, depth_count, sub_count, rows_here * channels)
    left_rows = lax.dynamic_index_in_dim(left_band, lax.axis_index("sub"), 2, keepdims=False)
    left_rows = left_rows.reshape(seq_group, depth_count * rows_here * channels)
    right_piece = dequantize(right_mantissa, right_exponent, piece_keep)
    projector = (
        out_weight.astype(jnp.float32).reshape(channels, channels, pair_channels) / total_seqs
    )
    own_start = lax.axis_index("depth") * rows_here
    gathered = lax.all_gather(right_piece, ("tile", "sub"), axis=1, tiled=True)
    terms = outer_block(left_rows, gathered, projector, rows_here)
    whole_sum = lax.psum(terms, "depth")
    summed = lax.dynamic_slice_in_dim(whole_sum, own_start, rows_here, 0)
    pair_rows = (summed + out_bias).astype(jnp.bfloat16)
    moved = transition(pair_rows, gate_weight, up_weight, down_weight)
    line_count = tile_count * depth_count
    split_view = moved.reshape(rows_here, line_count, sub_count, rows_here, pair_channels)
    received = lax.all_to_all(
        lax.all_to_all(split_view, ("tile", "depth"), split_axis=1, concat_axis=1, tiled=True),
        "sub",
        split_axis=2,
        concat_axis=2,
        tiled=True,
    )
    mirror = jnp.transpose(received, (3, 1, 2, 0, 4)).reshape(rows_here, residues, pair_channels)
    symmetric = ((moved.astype(jnp.float32) + mirror.astype(jnp.float32)) * 0.5).astype(
        jnp.bfloat16
    )
    logits = (
        jnp.dot(symmetric, distogram_weight, preferred_element_type=jnp.float32) + distogram_bias
    )
    return (
        symmetric.reshape(rows_here, residues * pair_channels),
        logits.reshape(rows_here, residues * distogram_weight.shape[1]),
    )


def solution(mesh):
    in_specs = (
        P(("parts", "depth"), "tile"),
        P(("parts", "depth"), "tile"),
        P(("parts", "depth"), ("tile", "sub")),
        P(("parts", "depth"), ("tile", "sub")),
        P("parts"),
        P(),
        P(),
        P(),
        P(),
        P(),
        P(),
        P(),
    )
    out_specs = (
        P(("parts", "tile", "depth", "sub"), None),
        P(("parts", "tile", "depth", "sub"), None),
    )
    return jax.shard_map(
        per_device, mesh=mesh, in_specs=in_specs, out_specs=out_specs, check_vma=False
    )
```

profile of v0, /device:TPU:0, one launch (start us, length us, event | category | flops | bytes accessed | tf_op | source)
XLA Modules:
  0.0 49.4 jit_solution(7804923227860699964)
XLA Ops:
  0.6 0.0 copy-start
  0.6 0.0 copy-start.2
  0.7 0.0 copy-start.11
  0.7 0.0 copy-start.6
  0.7 0.0 copy-start.4
  0.7 0.0 copy-start.1
  0.7 0.7 %copy-done.2 = bf16[128,128]{1,0:T(8,128)(2,1)S(1)} copy-done((bf16[128,128]{1,0:T(8,128)(2,1)S(1)}, bf16[128,128]{1,0:T(8,128)(2,1)}, u32[]{:S(2)}) %copy-start.2) | copy-done | bytes 32792
  1.4 0.1 copy.21
  1.6 0.0 copy-done.11
  1.6 0.1 dynamic-slice_convert_fusion.1
  1.6 0.1 dynamic-slice_convert_fusion
  1.7 0.0 copy-done.6
  1.7 0.1 exponential_multiply_fusion.1
  1.8 0.0 copy-done.4
  1.8 15.7 %all_gather.3 = bf16[128,512]{0,1:T(8,128)(2,1)S(1)} all-gather(bf16[128,64]{0,1:T(8,128)(2,1)S(1)} %fusion.10), channel_id=1, replica_groups=mesh['parts'=2,'tile'=4,'depth'=2,'sub'=2] {'tile','sub'}, dimensions={1}, use_global_device_ids=true | all-gather | bytes 147456 | tf_op jit(solution)/shard_map/all_gather | solution.py:94
  17.5 0.1 copy.23
  17.7 0.0 copy-done.1
  17.7 0.0 copy-start.5
  17.7 0.7 %copy-done.5 = s32[128,4]{0,1:T(4,128)S(1)} copy-done((s32[128,4]{0,1:T(4,128)S(1)}, s32[128,4]{0,1:T(4,128)}, u32[]{:S(2)}) %copy-start.5) | copy-done | bytes 2072
  18.4 0.1 exponential_multiply_fusion
  18.5 0.0 copy-start.9
  18.5 0.0 copy-start.10
  18.5 4.6 %while.10 = (s32[]{:T(128)}, f32[2,1,16,128]{3,2,1,0:T(8,128)S(1)}, s32[2]{0:T(128)S(1)}, bf16[128,64]{0,1:T(8,128)(2,1)S(1)}, bf16[128,512]{1,0:T(8,128)(2,1)S(...) while((s32[]{:T(128)}, f32[2,1,16,128]{3,2,1,0:T(8,128)S(1)}, ...), condition=%wide.region_1.2_spmd, body=%wide.region_0.1_spmd.sunk | while | flops 29360132 | bytes 1130663 | solution.py:48
  18.5 0.6 %dynamic_slice.35 = s32[1]{0:T(128)} dynamic-slice(s32[2]{0:T(128)S(1)} %get-tuple-element.120, s32[]{:T(128)} %get-tuple-element.108), dynamic_slice_sizes={1} | dynamic-slice | bytes 12 | tf_op jit(solution)/shard_map/while/body/jit(dynamic_index_in_dim)/dynamic_slice | solution.py:48
  19.8 0.1 fusion.52
  19.9 0.1 reshape.132
  20.0 0.8 %fusion.53 = f32[2,1,16,128]{3,2,1,0:T(8,128)S(1)} fusion(f32[2,1,16,128]{3,2,1,0:T(8,128)S(1)} %get-tuple-element.109, s32[]{:T(128)} %get-tuple-element.108, f32[32,16,32]{2,1,0:T(8,128)S(1)} %reshape.132, f32[32,32,128]{2,1,0:T(8,128)S(1)} %get-tuple-element.123), kind=kOutput, calls=%fused_computation.1.clone.1 | convolution fusion | flops 25165824 | bytes 794628 | tf_op jit(solution)/shard_map/while/body/eval_jaxpr/icje,cek->ijk/dot_general | solution.py:46
  20.8 0.6 %dynamic_slice.35 = s32[1]{0:T(128)} dynamic-slice(s32[2]{0:T(128)S(1)} %get-tuple-element.120, s32[]{:T(128)} %get-tuple-element.108), dynamic_slice_sizes={1} | dynamic-slice | bytes 12 | tf_op jit(solution)/shard_map/while/body/jit(dynamic_index_in_dim)/dynamic_slice | solution.py:48
  22.1 0.1 fusion.52
  22.2 0.1 reshape.132
  22.3 0.8 %fusion.53 = f32[2,1,16,128]{3,2,1,0:T(8,128)S(1)} fusion(f32[2,1,16,128]{3,2,1,0:T(8,128)S(1)} %get-tuple-element.109, s32[]{:T(128)} %get-tuple-element.108, f32[32,16,32]{2,1,0:T(8,128)S(1)} %reshape.132, f32[32,32,128]{2,1,0:T(8,128)S(1)} %get-tuple-element.123), kind=kOutput, calls=%fused_computation.1.clone.1 | convolution fusion | flops 25165824 | bytes 794628 | tf_op jit(solution)/shard_map/while/body/eval_jaxpr/icje,cek->ijk/dot_general | solution.py:46
  23.1 8.1 %psum.7 = f32[2,16,128]{2,1,0:T(8,128)S(1)} all-reduce(f32[2,16,128]{2,1,0:T(8,128)S(1)} %bitcast.63), channel_id=1, replica_groups=mesh['parts'=2,'tile'=4,'depth'=2,'sub'=2] {'depth'}, use_global_device_ids=true, to_apply=%region_2.3 | all-reduce | flops 4096 | bytes 32768 | tf_op jit(solution)/shard_map/psum | solution.py:96
  31.2 0.0 copy-start.8
  31.2 0.7 %copy-done.8 = f32[128]{0:T(128)S(1)} copy-done((f32[128]{0:T(128)S(1)}, f32[128]{0:T(128)}, u32[]{:S(2)}) %copy-start.8) | copy-done | bytes 536
  31.9 0.1 convert_reduce_fusion
  32.0 0.2 fusion.19
  32.2 0.0 copy-done
  32.2 0.2 fusion.24
  32.4 0.0 copy-done.9
  32.4 0.0 copy-done.10
  32.4 0.3 fusion.8
  32.7 10.9 %all_to_all.10 = bf16[1,8,2,1,128]{4,2,3,0,1:T(2,128)(2,1)S(1)} all-to-all(bf16[1,8,2,1,128]{4,2,3,0,1:T(2,128)(2,1)S(1)} %bitcast.62), channel_id=1, replica_groups=mesh['parts'=2,'tile'=4,'depth'=2,'sub'=2] {'tile','depth'}, dimensions={1} | all-to-all | bytes 8192 | tf_op jit(solution)/shard_map/all_to_all | solution.py:103
  43.6 3.7 %all_to_all.11 = bf16[1,8,2,1,128]{4,1,3,0,2:T(8,128)(2,1)S(1)} all-to-all(bf16[1,8,2,1,128]{4,1,3,0,2:T(8,128)(2,1)S(1)} %copy.25), channel_id=1, replica_groups=mesh['parts'=2,'tile'=4,'depth'=2,'sub'=2] {'sub'}, dimensions={2} | all-to-all | bytes 8192 | tf_op jit(solution)/shard_map/all_to_all | solution.py:102
  47.3 0.7 %copy-done.3 = bf16[128,64]{0,1:T(8,128)(2,1)S(1)} copy-done((bf16[128,64]{0,1:T(8,128)(2,1)S(1)}, bf16[128,64]{0,1:T(8,128)(2,1)}, u32[]{:S(2)}) %copy-start.3) | copy-done | bytes 16408
  48.0 0.0 copy-done.7
  48.0 0.1 convolution_add_fusion
  48.1 0.7 %reshape.126 = f32[1,1024]{1,0:T(1,128)} reshape(f32[16,64]{1,0:T(8,128)S(1)} %convolution_add_fusion) | data formatting | bytes 8192 | tf_op jit(solution)/shard_map/reshape | solution.py:118
  48.8 0.6 %copy.30 = bf16[1,1,16,128]{3,1,2,0:T(2,128)(2,1)} copy(bf16[1,1,16,128]{3,2,1,0:T(8,128)(2,1)S(1)} %fusion.34) | data formatting | bytes 8192
  (13 shorter events, 0.1 us)
Async XLA Ops:
  0.6 31.6 %copy-start = (bf16[128,512]{1,0:T(8,128)(2,1)S(1)}, bf16[128,512]{1,0:T(8,128)(2,1)}, u32[]{:S(2)}) copy-start(bf16[128,512]{1,0:T(8,128)(2,1)} %param.21) | copy-start | bytes 393220
  0.6 0.8 %copy-start.2 = (bf16[128,128]{1,0:T(8,128)(2,1)S(1)}, bf16[128,128]{1,0:T(8,128)(2,1)}, u32[]{:S(2)}) copy-start(bf16[128,128]{1,0:T(8,128)(2,1)} %param.14) | copy-start | bytes 98308
  0.7 0.9 %copy-start.11 = (s32[16]{0:T(128)S(1)}, s32[16]{0:T(128)}, u32[]{:S(2)}) copy-start(s32[16]{0:T(128)} %param.18) | copy-start | bytes 196
  0.7 1.0 %copy-start.6 = (s32[128,2]{0,1:T(2,128)S(1)}, s32[128,2]{0,1:T(2,128)}, u32[]{:S(2)}) copy-start(s32[128,2]{0,1:T(2,128)} %param.17) | copy-start | bytes 3076
  0.7 1.1 %copy-start.4 = (bf16[128,64]{0,1:T(8,128)(2,1)S(1)}, bf16[128,64]{0,1:T(8,128)(2,1)}, u32[]{:S(2)}) copy-start(bf16[128,64]{0,1:T(8,128)(2,1)} %param.16) | copy-start | bytes 49156
  0.7 17.0 %copy-start.1 = (bf16[1024,128]{1,0:T(8,128)(2,1)S(1)}, bf16[1024,128]{1,0:T(8,128)(2,1)}, u32[]{:S(2)}) copy-start(bf16[1024,128]{1,0:T(8,128)(2,1)} %param.19) | copy-start | bytes 786436
  17.7 0.7 %copy-start.5 = (s32[128,4]{0,1:T(4,128)S(1)}, s32[128,4]{0,1:T(4,128)}, u32[]{:S(2)}) copy-start(s32[128,4]{0,1:T(4,128)} %param.15) | copy-start | bytes 6148
  18.5 13.9 %copy-start.9 = (bf16[512,128]{1,0:T(8,128)(2,1)S(1)}, bf16[512,128]{1,0:T(8,128)(2,1)}, u32[]{:S(2)}) copy-start(bf16[512,128]{1,0:T(8,128)(2,1)} %param.23) | copy-start | bytes 393220
  18.5 13.9 %copy-start.10 = (bf16[128,512]{1,0:T(8,128)(2,1)S(1)}, bf16[128,512]{1,0:T(8,128)(2,1)}, u32[]{:S(2)}) copy-start(bf16[128,512]{1,0:T(8,128)(2,1)} %param.22) | copy-start | bytes 393220
  31.2 0.7 %copy-start.8 = (f32[128]{0:T(128)S(1)}, f32[128]{0:T(128)}, u32[]{:S(2)}) copy-start(f32[128]{0:T(128)} %param.20) | copy-start | bytes 1540
  47.3 0.7 %copy-start.3 = (bf16[128,64]{0,1:T(8,128)(2,1)S(1)}, bf16[128,64]{0,1:T(8,128)(2,1)}, u32[]{:S(2)}) copy-start(bf16[128,64]{0,1:T(8,128)(2,1)} %param.24) | copy-start | bytes 49156
  47.3 0.7 %copy-start.7 = (f32[64]{0:T(128)S(1)}, f32[64]{0:T(128)}, u32[]{:S(2)}) copy-start(f32[64]{0:T(128)} %param.25) | copy-start | bytes 772
where the time goes:
time: 49.8 us; the launch traced here: 49.4 us
  blocking collectives  38.5 us (77%)
  local copies, waits for them, and re-layouts  5.73 us (12%)
  matrix products  2.43 us (5%)
  loops' own time  1.34 us (3%)
  between operations  0.82 us (2%)
  other arithmetic  0.66 us (1%)
    all_gather x1, blocking collectives, per_device(): gathered = lax.all_gather(right_piece, ('tile', 'sub'), axis=1, tiled=True)  15.7 us
    all_to_all x1, blocking collectives, per_device(): lax.all_to_all(split_view, ('tile', 'depth'), split_axis=1, concat_axis=1...  10.9 us
    psum x1, blocking collectives, per_device(): whole_sum = lax.psum(terms, 'depth')  8.14 us
    all_to_all x1, blocking collectives, per_device(): lax.all_to_all(lax.all_to_all(split_view, ('tile', 'depth'), split_axis=1...  3.69 us
    unnamed x26, local copies, waits for them, and re-layouts  3.5 us
    dot_general x2, matrix products, one_block(): jnp.einsum('icje,cek->ijk', outer, projector, precision=lax.Precision.HIG...  1.55 us
    another operation x1, loops' own time, outer_block(): blocks = lax.map(one_block, jnp.arange(block_count, dtype=jnp.int32))  1.34 us
    dynamic_slice x2, local copies, waits for them, and re-layouts, outer_block(): blocks = lax.map(one_block, jnp.arange(block_count, dtype=jnp.int32))  1.18 us

commit v1 on v0

v1 whole, which is shorter than its diff:
```python
import functools

import jax
import jax.numpy as jnp
from jax import lax
from jax.experimental import pallas as pl
from jax.experimental.pallas import tpu as pltpu
from jax.sharding import PartitionSpec as P


LANES = 128
ROWS = 8
GROUP = ("tile", "depth", "sub")
NT = (((1,), (1,)), ((), ()))
VMEM = pl.BlockSpec(memory_space=pltpu.VMEM)
SMEM = pl.BlockSpec(memory_space=pltpu.SMEM)


def parity(number):
    return bin(number).count("1") & 1


def xor_permute(value, tile_bits, depth_bits, sub_bits):
    depth_count, sub_count = lax.axis_size("depth"), lax.axis_size("sub")
    pairs = []
    for t in range(lax.axis_size("tile")):
        for d in range(depth_count):
            for s in range(sub_count):
                here = (t * depth_count + d) * sub_count + s
                there = ((t ^ tile_bits) * depth_count + (d ^ depth_bits)) * sub_count + (s ^ sub_bits)
                pairs.append((here, there))
    return lax.ppermute(value, GROUP, pairs)


def bits_of(count):
    return [1 << b for b in reversed(range(count.bit_length() - 1))]


def row_in_tile(sub_count):
    return lax.axis_index("depth") * sub_count + lax.axis_index("sub")


def prepare_kernel(
    dims, left_ref, left_exp_ref, right_ref, right_exp_ref, mask_ref, block_ref, left_out, right_out, left_f32
):
    channels, _, sub_count = dims
    band = left_exp_ref.shape[0]
    piece = right_exp_ref.shape[0]
    fold = channels // ROWS
    tile, sub = lax.axis_index("tile"), lax.axis_index("sub")
    mine = row_in_tile(sub_count)
    right = right_ref[...].astype(jnp.float32)
    right_scale = jnp.exp2(right_exp_ref[...].astype(jnp.float32))
    first = tile * band + sub * piece
    scaled = []
    for j in range(piece):
        scale = right_scale[j : j + 1] * mask_ref[first + j].astype(jnp.float32)
        scaled.append(right[j * channels : (j + 1) * channels] * scale)
        right_out[j * channels : (j + 1) * channels, :] = scaled[j].astype(jnp.bfloat16)
    half = fold * piece * ROWS
    for x in range(fold):
        rows = jnp.concatenate([scaled[j][x * ROWS : (x + 1) * ROWS] for j in range(piece)], axis=0)
        at = half + x * piece * ROWS
        block_ref[at : at + piece * ROWS, :] = rows.astype(jnp.bfloat16)
    left = jnp.transpose(left_ref[...].astype(jnp.float32))
    left_scale = jnp.exp2(left_exp_ref[...].astype(jnp.float32))
    for i in range(band):
        scale = left_scale[i : i + 1] * mask_ref[tile * band + i].astype(jnp.float32)
        left_f32[i * channels : (i + 1) * channels, :] = left[i * channels : (i + 1) * channels] * scale
    for x in range(fold):
        rows = []
        for j in range(piece):
            at = pl.multiple_of((sub * piece + j) * channels + x * ROWS, ROWS)
            rows.append(left_f32[pl.ds(at, ROWS), :])
        at = x * piece * ROWS
        block_ref[at : at + piece * ROWS, :] = jnp.concatenate(rows, axis=0).astype(jnp.bfloat16)
    for i in range(band):
        at = pl.multiple_of((mine ^ i) * channels, channels)
        left_out[i * channels : (i + 1) * channels, :] = left_f32[pl.ds(at, channels), :].astype(jnp.bfloat16)


def spread_kernel(
    dims, left_ref, right_ref, other_ref, weight_ref, left_spread, right_spread, weight_out, both, weight_f32
):
    channels, _, sub_count = dims
    seqs = left_ref.shape[1]
    band = left_ref.shape[0] // channels
    piece = right_ref.shape[0] // channels
    fold = channels // ROWS
    sub = lax.axis_index("sub")
    mine = row_in_tile(sub_count)
    both[sub] = right_ref[...].reshape(piece, channels, seqs)
    both[1 - sub] = other_ref[...].reshape(piece, channels, seqs)
    left_spread[...] = jnp.zeros_like(left_spread)
    right_spread[...] = jnp.zeros_like(right_spread)
    for i in range(band):
        here = mine ^ i
        left = left_ref[i * channels : (i + 1) * channels, :]
        right = both[here // piece, here % piece]
        for x in range(fold):
            at = (i * fold + x) * channels
            left_spread[at : at + channels, x * seqs : (x + 1) * seqs] = left
            right_spread[at : at + channels, x * seqs : (x + 1) * seqs] = right
    weight_f32[...] = weight_ref[...].astype(jnp.float32)
    for g in range(ROWS):
        for x in range(fold):
            at = (g * fold + x) * channels
            rows = weight_f32[pl.ds(x * ROWS + g, channels, stride=channels), :]
            weight_out[at : at + channels, :] = rows.astype(jnp.bfloat16)


def pair_kernel(dims, block_count, *refs):
    channels, _, sub_count = dims
    blocks = refs[:block_count]
    left_spread, right_spread, weight_ref, swapped_ref, keep_ref, core_ref, chip_ref, outer = refs[block_count:]
    fold = channels // ROWS
    half = blocks[0].shape[0] // 2
    size = half // fold
    piece = size // ROWS
    count = block_count * piece
    band = left_spread.shape[0] // (fold * channels)
    width = fold * channels
    natural = jnp.concatenate(
        [
            weight_ref[(x * ROWS + g) * channels : (x * ROWS + g + 1) * channels, :]
            for g in range(ROWS)
            for x in range(fold)
        ],
        axis=0,
    )
    for way in range(2):
        base = half * (1 - way)
        factor = jnp.concatenate(
            [
                jnp.concatenate([b[base + x * size : base + (x + 1) * size, :] for b in blocks], axis=0)
                for x in range(fold)
            ],
            axis=1,
        )
        spread = left_spread if way == 0 else right_spread
        product = lax.dot_general(factor, spread[...], NT, preferred_element_type=jnp.float32)
        for i in range(band):
            outer[way * band + i] = product[:, i * width : (i + 1) * width]
        flat = jnp.concatenate(
            [
                jnp.concatenate(
                    [outer[way * band + i, pl.ds(g, count, stride=ROWS), :] for g in range(ROWS)],
                    axis=1,
                )
                for i in range(band)
            ],
            axis=0,
        )
        high = flat.astype(jnp.bfloat16)
        low = (flat - high.astype(jnp.float32)).astype(jnp.bfloat16)
        weight = swapped_ref[...] if way == 0 else natural
        terms = jnp.dot(jnp.concatenate([high, low], axis=0), weight, preferred_element_type=jnp.float32)
        terms = terms[: band * count] + terms[band * count :]
        place = lambda i: slice(i * count, (i + 1) * count)
        keep_ref[place(way), :] = terms[place(0)]
        core_ref[place(way), :] = terms[place(1)]
        for i in range(sub_count, band):
            chip_ref[place((i - sub_count) * 2 + way), :] = terms[place(i)]


def finish_kernel(
    dims,
    block_tiles,
    total_seqs,
    keep_ref,
    core_ref,
    chip_ref,
    relay_ref,
    out_bias,
    gate_weight,
    up_weight,
    down_weight,
    bins_weight,
    bins_bias,
    symmetric_out,
    bins_out,
):
    _, depth_count, sub_count = dims
    pair_channels = gate_weight.shape[0]
    bins = bins_weight.shape[0]
    count = keep_ref.shape[0] // 2
    piece = count // len(block_tiles)
    band = piece * sub_count
    tile, sub = lax.axis_index("tile"), lax.axis_index("sub")
    if depth_count > 1:
        here = keep_ref[...] + relay_ref[: 2 * count, :]
        there = core_ref[...] + chip_ref[2 * count :, :]
    else:
        here, there = keep_ref[...], core_ref[...]
    summed = jnp.concatenate([here[:count], there[:count], here[count:], there[count:]], axis=0)
    pair = (summed * (1.0 / total_seqs) + out_bias[...]).astype(jnp.bfloat16)
    values = pair.astype(jnp.float32)
    center = jnp.mean(values, axis=-1, keepdims=True)
    shifted = values - center
    spread = jnp.mean(shifted * shifted, axis=-1, keepdims=True)
    normed = (shifted * lax.rsqrt(spread + 1e-05)).astype(jnp.bfloat16)
    gate = jnp.dot(normed, gate_weight[...], preferred_element_type=jnp.float32)
    up = jnp.dot(normed, up_weight[...], preferred_element_type=jnp.float32)
    hidden = (jax.nn.silu(gate) * up).astype(jnp.bfloat16)
    moved = (values + jnp.dot(hidden, down_weight[...], preferred_element_type=jnp.float32)).astype(jnp.bfloat16)
    moved = moved.astype(jnp.float32)
    symmetric = ((moved[: 2 * count] + moved[2 * count :]) * 0.5).astype(jnp.bfloat16)
    packed = LANES // bins
    weight = jnp.concatenate([bins_weight[...]] * packed, axis=0)
    bias = jnp.concatenate([bins_bias[...]] * packed, axis=1)
    logits = lax.dot_general(symmetric, weight, NT, preferred_element_type=jnp.float32) + bias
    lane = lax.broadcasted_iota(jnp.int32, (1, LANES), 1)
    symmetric = symmetric.astype(jnp.float32)
    for side in range(2):
        for k, bits in enumerate(block_tiles):
            half = sub ^ (parity(bits) ^ side)
            start = (tile ^ bits) * band + half * piece
            row = side * count + k * piece
            for j in range(piece):
                at = pl.multiple_of((start + j) * pair_channels, pair_channels)
                symmetric_out[:, pl.ds(at, pair_channels)] = symmetric[row + j : row + j + 1].astype(jnp.bfloat16)
            for j in range(0, piece, packed):
                line = logits[row + j : row + j + 1]
                for p in range(1, packed):
                    line = jnp.where(lane < p * bins, line, logits[row + j + p : row + j + p + 1])
                at = pl.multiple_of((start + j) * bins, LANES)
                bins_out[:, pl.ds(at, LANES)] = line


def cost(flops, size):
    return pl.CostEstimate(flops=flops, bytes_accessed=size, transcendentals=0)


def shape(rows, columns, kind):
    return jax.ShapeDtypeStruct((rows, columns), kind)


def per_device(
    left_mantissa,
    left_exponent,
    right_mantissa,
    right_exponent,
    residue_mask,
    out_weight,
    out_bias,
    gate_weight,
    up_weight,
    down_weight,
    distogram_weight,
    distogram_bias,
):
    tile_count, depth_count, sub_count = (lax.axis_size(a) for a in GROUP)
    seqs, width = left_mantissa.shape
    band = left_exponent.shape[1]
    piece = right_exponent.shape[1]
    channels = width // band
    fold = channels // ROWS
    residues = residue_mask.shape[0]
    pair_channels = out_weight.shape[1]
    bins = distogram_weight.shape[1]
    if sub_count != 2 or band != depth_count * sub_count or tile_count & (tile_count - 1) or band & (band - 1):
        raise ValueError("unsupported mesh")
    dims = (channels, depth_count, sub_count)
    bf16, f32 = jnp.bfloat16, jnp.float32

    own, left_rows, right_rows = pl.pallas_call(
        functools.partial(prepare_kernel, dims),
        out_shape=(
            shape(2 * piece * channels, seqs, bf16),
            shape(band * channels, seqs, bf16),
            shape(piece * channels, seqs, bf16),
        ),
        in_specs=[VMEM] * 4 + [SMEM],
        out_specs=(VMEM,) * 3,
        scratch_shapes=[pltpu.VMEM((band * channels, seqs), f32)],
        cost_estimate=cost(1 << 16, 1 << 17),
        name="prepare",
    )(left_mantissa, left_exponent.T, right_mantissa.T, right_exponent.T, residue_mask)
    blocks = {0: own}
    for bit in bits_of(tile_count):
        for bits in list(blocks):
            blocks[bits ^ bit] = xor_permute(blocks[bits], bit, 0, 1)
    other_rows = xor_permute(right_rows, 0, 0, 1)
    left_spread, right_spread, swapped = pl.pallas_call(
        functools.partial(spread_kernel, dims),
        out_shape=(
            shape(band * fold * channels, fold * seqs, bf16),
            shape(band * fold * channels, fold * seqs, bf16),
            shape(*out_weight.shape, bf16),
        ),
        in_specs=[VMEM] * 4,
        out_specs=(VMEM,) * 3,
        scratch_shapes=[pltpu.VMEM((sub_count, piece, channels, seqs), bf16), pltpu.VMEM(out_weight.shape, f32)],
        cost_estimate=cost(1 << 16, 1 << 20),
        name="spread",
    )(left_rows, right_rows, other_rows, out_weight)
    block_tiles = tuple(sorted(blocks))
    count = len(block_tiles) * piece
    keep, core, chip = pl.pallas_call(
        functools.partial(pair_kernel, dims, len(block_tiles)),
        out_shape=(
            shape(2 * count, pair_channels, f32),
            shape(2 * count, pair_channels, f32),
            shape(max(band - sub_count, 1) * 2 * count, pair_channels, f32),
        ),
        in_specs=[VMEM] * (len(block_tiles) + 4),
        out_specs=(VMEM,) * 3,
        scratch_shapes=[pltpu.VMEM((2 * band, count * ROWS, fold * channels), f32)],
        cost_estimate=cost(1 << 27, 1 << 21),
        name="pair",
    )(*(blocks[k] for k in block_tiles), left_spread, right_spread, out_weight, swapped)
    size = sub_count * 2 * count
    for bit in bits_of(depth_count)[:-1]:
        rows = jnp.concatenate([keep, core, chip], axis=0)
        rows = rows.reshape(-1, 2, bit, size // sub_count * sub_count, pair_channels)[0]
        mine = rows[0] + xor_permute(rows[1], 0, bit, 0)
        mine = mine.reshape(-1, pair_channels)
        keep, core, chip = mine[: size // 2], mine[size // 2 : size], mine[size:]
    from_chip = xor_permute(chip, 0, 1, 1) if depth_count > 1 else chip
    from_core = xor_permute(core, 0, 0, 1)
    relayed = xor_permute(from_chip[: 2 * count], 0, 0, 1) if depth_count > 1 else from_core
    return pl.pallas_call(
        functools.partial(finish_kernel, dims, block_tiles, seqs * depth_count),
        out_shape=(shape(1, residues * pair_channels, bf16), shape(1, residues * bins, f32)),
        in_specs=[VMEM] * 10,
        out_specs=(VMEM, VMEM),
        cost_estimate=cost(1 << 25, 1 << 20),
        name="finish",
    )(
        keep,
        from_core,
        from_chip,
        relayed,
        out_bias.reshape(1, -1),
        gate_weight,
        up_weight,
        down_weight,
        distogram_weight.T,
        distogram_bias.reshape(1, -1),
    )


def solution(mesh):
    in_specs = (
        P(("parts", "depth"), "tile"),
        P(("parts", "depth"), "tile"),
        P(("parts", "depth"), ("tile", "sub")),
        P(("parts", "depth"), ("tile", "sub")),
        P("parts"),
        P(),
        P(),
        P(),
        P(),
        P(),
        P(),
        P(),
    )
    out_specs = (
        P(("parts", "tile", "depth", "sub"), None),
        P(("parts", "tile", "depth", "sub"), None),
    )
    step = jax.shard_map(
        per_device, mesh=mesh, in_specs=in_specs, out_specs=out_specs, check_vma=False
    )
    known = [0]
    for bit in bits_of(mesh.shape["tile"]):
        for bits in list(known):
            known.append(bits ^ bit)
    return step
```

time: 49.8 us -> 25 us (0.50)
  blocking collectives: 38.5 us -> 0 us
  starting transfers between devices: 0 us -> 9.31 us
  Pallas kernels: 0 us -> 8.85 us
  waiting for transfers between devices: 0 us -> 4.15 us
  local copies, waits for them, and re-layouts: 5.73 us -> 1.8 us
  matrix products: 2.43 us -> 0 us
  loops' own time: 1.34 us -> 0 us
  other arithmetic: 0.66 us -> 0 us
    all_gather x1 -> x0, blocking collectives: 15.7 us -> none  [per_device(): gathered = lax.all_gather(right_piece, ('tile', 'sub'), axis=1, tiled=True)]
    all_to_all x2 -> x0, blocking collectives: 14.6 us -> none  [the longest x1 10.9 us: per_device(): lax.all_to_all(split_view, ('tile', 'depth'), split_axis=1, concat_axis=1...]
    ppermute x0 -> x7, starting transfers between devices: none -> 9.31 us  [xor_permute(): return lax.ppermute(value, GROUP, pairs)]
    pallas_call x0 -> x4, Pallas kernels: none -> 8.85 us  [the longest x1 2.8 us: per_device(): pl.pallas_call(functools.partial(pair_kernel, dims, len(block_tiles)), ou...]
    psum x1 -> x0, blocking collectives: 8.14 us -> none  [per_device(): whole_sum = lax.psum(terms, 'depth')]
    ppermute x0 -> x7, waiting for transfers between devices: none -> 4.15 us  [xor_permute(): return lax.ppermute(value, GROUP, pairs)]
    dot_general x7 -> x0, matrix products: 2.43 us -> none  [the longest x2 1.55 us: one_block(): jnp.einsum('icje,cek->ijk', outer, projector, precision=lax.Precision.HIG...]
    unnamed x26 -> x14, local copies, waits for them, and re-layouts: 3.5 us -> 1.79 us
  transfers between devices with their start and end apart: 0 -> 7, of which waited for: 0 -> 4; matrix products, arithmetic and copies ran while one was open for 0% -> 0% of each run, Pallas kernels for 0% -> 9%
where the time goes in v1:
time: 25 us; the launch traced here: 24.8 us
  starting transfers between devices  9.31 us (37%)
  Pallas kernels  8.85 us (35%)
  waiting for transfers between devices  4.15 us (17%)
  local copies, waits for them, and re-layouts  1.8 us (7%)
  between operations  0.67 us (3%)
    ppermute x7, starting transfers between devices, xor_permute(): return lax.ppermute(value, GROUP, pairs)  9.31 us
    ppermute x7, waiting for transfers between devices, xor_permute(): return lax.ppermute(value, GROUP, pairs)  4.15 us
    pallas_call x1, Pallas kernels, per_device(): pl.pallas_call(functools.partial(pair_kernel, dims, len(block_tiles)), ou...  2.8 us
    pallas_call x1, Pallas kernels, per_device(): pl.pallas_call(functools.partial(finish_kernel, dims, block_tiles, seqs *...  2.29 us
    pallas_call x1, Pallas kernels, per_device(): pl.pallas_call(functools.partial(spread_kernel, dims), out_shape=(shape(b...  2.21 us
    unnamed x14, local copies, waits for them, and re-layouts  1.79 us
    pallas_call x1, Pallas kernels, per_device(): pl.pallas_call(functools.partial(prepare_kernel, dims), out_shape=(shape(...  1.54 us
  transfers between devices with their start and end apart: 7, of which 4 were waited for; matrix products, arithmetic and copies ran while one was open for 0% of the time, Pallas kernels for 9%

profile of v1, /device:TPU:0, one launch (start us, length us, event | category | flops | bytes accessed | tf_op | source)
XLA Modules:
  0.0 24.8 jit_solution(4081484458300077728)
XLA Ops:
  0.6 1.5 %prepare.1 = (bf16[128,128]{1,0:T(8,128)(2,1)}, bf16[128,128]{1,0:T(8,128)(2,1)}, bf16[64,128]{1,0:T(8,128)(2,1)}) custom-call(bf16[128,128]{1,0:T(8,128)(2,1)} %left_ref.1, s32[4,128]{1,0:T(4,128)} %bitcast.8, bf16[64,128]{1,0:T(8,128)(2,1)} %bitcast.7, s32[2,128]{1,0:T(2,128)} %bitcast.9, s32[16]{0:T(128)} %mask_ref.1), custom_call_target="tpu_custom_call" | custom-call | flops 65536 | bytes 131072 | tf_op jit(solution)/shard_map/prepare/pallas_call | solution.py:266
  2.2 3.5 %collective-permute-start.1 = (bf16[128,128]{1,0:T(8,128)(2,1)}, bf16[128,128]{1,0:T(8,128)(2,1)S(1)}, u32[]{:S(2)}, u32[]{:S(2)}) collective-permute-start(bf16[128,128]{1,0:T(8,128)(2,1)} %get-tuple-element.11.refs_0_), channel_id=1, source_target_pairs={{0,9},{1,8},{2,11},{3,10},{4,13},{5,12},{6,15},{7,14},{8,1},{9,0},... | collective-permute-start | bytes 98312 | tf_op jit(solution)/shard_map/ppermute | solution.py:32
  5.7 1.9 %collective-permute-start = (bf16[128,128]{1,0:T(8,128)(2,1)}, bf16[128,128]{1,0:T(8,128)(2,1)S(1)}, u32[]{:S(2)}, u32[]{:S(2)}) collective-permute-start(bf16[128,128]{1,0:T(8,128)(2,1)} %get-tuple-element.11.refs_0_), channel_id=1, source_target_pairs={{0,5},{1,4},{2,7},{3,6},{4,1},{5,0},{6,3},{7,2},{8,13},{9,12},{10,... | collective-permute-start | bytes 98312 | tf_op jit(solution)/shard_map/ppermute | solution.py:32
  7.5 0.2 collective-permute-done.1.refs_2_
  7.8 0.0 copy-start.1
  7.8 1.9 %collective-permute-start.2 = (bf16[128,128]{1,0:T(8,128)(2,1)S(1)}, bf16[128,128]{1,0:T(8,128)(2,1)S(1)}, u32[]{:S(2)}, u32[]{:S(2)}) collective-permute-start(bf16[128,128]{1,0:T(8,128)(2,1)S(1)} %collective-permute-done.1.refs_2_), channel_id=1, source_target_pairs={{0,5},{1,4},{2,7},{3,6},{4,1},{5,0},{6,3},{7,2},{8,13},{9,12},{10,... | collective-permute-start | bytes 98312 | tf_op jit(solution)/shard_map/ppermute | solution.py:32
  9.7 0.2 collective-permute-start.3
  9.9 1.2 %collective-permute-done.3.other_ref = bf16[64,128]{1,0:T(8,128)(2,1)S(1)} collective-permute-done((bf16[64,128]{1,0:T(8,128)(2,1)}, bf16[64,128]{1,0:T(8,128)(2,1)S(1)}, u32[]{:S(2)}, u32[]{:S(2)}) %collective-permute-start.3) | collective-permute-done | bytes 16416 | tf_op jit(solution)/shard_map/ppermute | solution.py:32
  11.1 0.0 copy-start.4
  11.1 0.6 %copy-done.4 = bf16[64,128]{1,0:T(8,128)(2,1)} copy-done((bf16[64,128]{1,0:T(8,128)(2,1)}, bf16[64,128]{1,0:T(8,128)(2,1)S(1)}, u32[]{:S(2)}) %copy-start.4) | copy-done | bytes 16408
  11.7 2.2 %spread.1 = (bf16[512,512]{1,0:T(8,128)(2,1)}, bf16[512,512]{1,0:T(8,128)(2,1)}, bf16[1024,128]{1,0:T(8,128)(2,1)}) custom-call(bf16[128,128]{1,0:T(8,128)(2,1)} %get-tuple-element.12.left_ref, bf16[64,128]{1,0:T(8,128)(2,1)} %get-tuple-element.13.right_ref, bf16[64,128]{1,0:T(8,128)(2,1)} %copy-done.4, bf16[1024,128]{1,0:T(8,128)(2,1)} %refs_6_.1), custom_call_target="tpu_custom_call" | custom-call | flops 65536 | bytes 1048576 | tf_op jit(solution)/shard_map/spread/pallas_call | solution.py:284
  13.9 0.0 copy-done.1
  13.9 0.0 collective-permute-done.refs_1_
  13.9 0.0 copy-start.2
  13.9 0.0 collective-permute-done.2.refs_3_
  13.9 0.0 copy-start.3
  13.9 0.6 %copy-done.2 = bf16[128,128]{1,0:T(8,128)(2,1)} copy-done((bf16[128,128]{1,0:T(8,128)(2,1)}, bf16[128,128]{1,0:T(8,128)(2,1)S(1)}, u32[]{:S(2)}) %copy-start.2) | copy-done | bytes 32792
  14.5 0.0 copy-done.3
  14.5 2.8 %pair.1 = (f32[16,128]{1,0:T(8,128)}, f32[16,128]{1,0:T(8,128)}, f32[32,128]{1,0:T(8,128)}) custom-call(bf16[128,128]{1,0:T(8,128)(2,1)} %get-tuple-element.11.refs_0_, bf16[128,128]{1,0:T(8,128)(2,1)} %copy-done.2, bf16[128,128]{1,0:T(8,128)(2,1)} %copy-done.1, bf16[128,128]{1,0:T(8,128)(2,1)} %copy-done.3, bf16[512,512]{1,0:T(8,128)(2,1)} %get-tuple-element.14.refs_4_, ...), custom_call_target="tpu_custom_call" | custom-call | flops 134217728 | bytes 2097152 | tf_op jit(solution)/shard_map/pair/pallas_call | solution.py:299
  17.3 1.3 %collective-permute-start.5 = (f32[32,128]{1,0:T(8,128)}, f32[32,128]{1,0:T(8,128)S(1)}, u32[]{:S(2)}, u32[]{:S(2)}) collective-permute-start(f32[32,128]{1,0:T(8,128)} %get-tuple-element.19), channel_id=1, source_target_pairs={{0,3},{1,2},{2,1},{3,0},{4,7},{5,6},{6,5},{7,4},{8,11},{9,10},{10,... | collective-permute-start | bytes 49160 | tf_op jit(solution)/shard_map/ppermute | solution.py:32
  18.6 0.3 %collective-permute-start.4 = (f32[16,128]{1,0:T(8,128)}, f32[16,128]{1,0:T(8,128)S(1)}, u32[]{:S(2)}, u32[]{:S(2)}) collective-permute-start(f32[16,128]{1,0:T(8,128)} %get-tuple-element.18), channel_id=1, source_target_pairs={{0,1},{1,0},{2,3},{3,2},{4,5},{5,4},{6,7},{7,6},{8,9},{9,8},{10,11... | collective-permute-start | bytes 24584 | tf_op jit(solution)/shard_map/ppermute | solution.py:32
  18.9 1.8 %collective-permute-done.5.chip_ref = f32[32,128]{1,0:T(8,128)S(1)} collective-permute-done((f32[32,128]{1,0:T(8,128)}, f32[32,128]{1,0:T(8,128)S(1)}, u32[]{:S(2)}, u32[]{:S(2)}) %collective-permute-start.5) | collective-permute-done | bytes 16416 | tf_op jit(solution)/shard_map/ppermute | solution.py:32
  20.7 0.0 copy-start
  20.7 0.2 collective-permute-start.6
  20.9 0.0 collective-permute-done.4.core_ref
  20.9 0.0 copy-start.5
  20.9 1.0 %collective-permute-done.6.relay_ref = f32[16,128]{1,0:T(8,128)S(1)} collective-permute-done((f32[16,128]{1,0:T(8,128)S(1)}, f32[16,128]{1,0:T(8,128)S(1)}, u32[]{:S(2)}, u32[]{:S(2)}) %collective-permute-start.6) | collective-permute-done | bytes 8224 | tf_op jit(solution)/shard_map/ppermute | solution.py:32
  21.9 0.0 copy-start.6
  21.9 0.0 copy-done
  21.9 0.0 copy-done.5
  21.9 0.6 %copy-done.6 = f32[16,128]{1,0:T(8,128)} copy-done((f32[16,128]{1,0:T(8,128)}, f32[16,128]{1,0:T(8,128)S(1)}, u32[]{:S(2)}) %copy-start.6) | copy-done | bytes 8216
  22.5 2.3 %finish.1 = (bf16[1,2048]{1,0:T(2,128)(2,1)}, f32[1,1024]{1,0:T(1,128)}) custom-call(f32[16,128]{1,0:T(8,128)} %get-tuple-element.17.keep_ref, f32[16,128]{1,0:T(8,128)} %copy-done.5, f32[32,128]{1,0:T(8,128)} %copy-done, f32[16,128]{1,0:T(8,128)} %copy-done.6, f32[1,128]{1,0:T(1,128)} %bitcast.10, bf16[128,512]{1,0:T(8,128)(2,1)} %gate_weight.1, ...), custom_call_target="tpu_custom_call" | custom-call | flops 33554432 | bytes 1048576 | tf_op jit(solution)/shard_map/finish/pallas_call | solution.py:322
  (1 shorter events, 0.0 us)
Async XLA Ops:
  2.2 5.6 %collective-permute-start.1 = (bf16[128,128]{1,0:T(8,128)(2,1)}, bf16[128,128]{1,0:T(8,128)(2,1)S(1)}, u32[]{:S(2)}, u32[]{:S(2)}) collective-permute-start(bf16[128,128]{1,0:T(8,128)(2,1)} %get-tuple-element.11.refs_0_), channel_id=1, source_target_pairs={{0,9},{1,8},{2,11},{3,10},{4,13},{5,12},{6,15},{7,14},{8,1},{9,0},... | collective-permute-start | bytes 98312 | tf_op jit(solution)/shard_map/ppermute | solution.py:32
  5.7 8.2 %collective-permute-start = (bf16[128,128]{1,0:T(8,128)(2,1)}, bf16[128,128]{1,0:T(8,128)(2,1)S(1)}, u32[]{:S(2)}, u32[]{:S(2)}) collective-permute-start(bf16[128,128]{1,0:T(8,128)(2,1)} %get-tuple-element.11.refs_0_), channel_id=1, source_target_pairs={{0,5},{1,4},{2,7},{3,6},{4,1},{5,0},{6,3},{7,2},{8,13},{9,12},{10,... | collective-permute-start | bytes 98312 | tf_op jit(solution)/shard_map/ppermute | solution.py:32
  7.8 6.1 %copy-start.1 = (bf16[128,128]{1,0:T(8,128)(2,1)}, bf16[128,128]{1,0:T(8,128)(2,1)S(1)}, u32[]{:S(2)}) copy-start(bf16[128,128]{1,0:T(8,128)(2,1)S(1)} %collective-permute-done.1.refs_2_) | copy-start | bytes 98308
  7.8 6.1 %collective-permute-start.2 = (bf16[128,128]{1,0:T(8,128)(2,1)S(1)}, bf16[128,128]{1,0:T(8,128)(2,1)S(1)}, u32[]{:S(2)}, u32[]{:S(2)}) collective-permute-start(bf16[128,128]{1,0:T(8,128)(2,1)S(1)} %collective-permute-done.1.refs_2_), channel_id=1, source_target_pairs={{0,5},{1,4},{2,7},{3,6},{4,1},{5,0},{6,3},{7,2},{8,13},{9,12},{10,... | collective-permute-start | bytes 98312 | tf_op jit(solution)/shard_map/ppermute | solution.py:32
  9.7 1.4 %collective-permute-start.3 = (bf16[64,128]{1,0:T(8,128)(2,1)}, bf16[64,128]{1,0:T(8,128)(2,1)S(1)}, u32[]{:S(2)}, u32[]{:S(2)}) collective-permute-start(bf16[64,128]{1,0:T(8,128)(2,1)} %get-tuple-element.13.right_ref), channel_id=1, source_target_pairs={{0,1},{1,0},{2,3},{3,2},{4,5},{5,4},{6,7},{7,6},{8,9},{9,8},{10,11... | collective-permute-start | bytes 49160 | tf_op jit(solution)/shard_map/ppermute | solution.py:32
  11.1 0.6 %copy-start.4 = (bf16[64,128]{1,0:T(8,128)(2,1)}, bf16[64,128]{1,0:T(8,128)(2,1)S(1)}, u32[]{:S(2)}) copy-start(bf16[64,128]{1,0:T(8,128)(2,1)S(1)} %collective-permute-done.3.other_ref) | copy-start | bytes 49156
  13.9 0.6 %copy-start.2 = (bf16[128,128]{1,0:T(8,128)(2,1)}, bf16[128,128]{1,0:T(8,128)(2,1)S(1)}, u32[]{:S(2)}) copy-start(bf16[128,128]{1,0:T(8,128)(2,1)S(1)} %collective-permute-done.refs_1_) | copy-start | bytes 98308
  13.9 0.6 %copy-start.3 = (bf16[128,128]{1,0:T(8,128)(2,1)}, bf16[128,128]{1,0:T(8,128)(2,1)S(1)}, u32[]{:S(2)}) copy-start(bf16[128,128]{1,0:T(8,128)(2,1)S(1)} %collective-permute-done.2.refs_3_) | copy-start | bytes 98308
  17.3 3.4 %collective-permute-start.5 = (f32[32,128]{1,0:T(8,128)}, f32[32,128]{1,0:T(8,128)S(1)}, u32[]{:S(2)}, u32[]{:S(2)}) collective-permute-start(f32[32,128]{1,0:T(8,128)} %get-tuple-element.19), channel_id=1, source_target_pairs={{0,3},{1,2},{2,1},{3,0},{4,7},{5,6},{6,5},{7,4},{8,11},{9,10},{10,... | collective-permute-start | bytes 49160 | tf_op jit(solution)/shard_map/ppermute | solution.py:32
  18.6 2.3 %collective-permute-start.4 = (f32[16,128]{1,0:T(8,128)}, f32[16,128]{1,0:T(8,128)S(1)}, u32[]{:S(2)}, u32[]{:S(2)}) collective-permute-start(f32[16,128]{1,0:T(8,128)} %get-tuple-element.18), channel_id=1, source_target_pairs={{0,1},{1,0},{2,3},{3,2},{4,5},{5,4},{6,7},{7,6},{8,9},{9,8},{10,11... | collective-permute-start | bytes 24584 | tf_op jit(solution)/shard_map/ppermute | solution.py:32
  20.7 1.2 %copy-start = (f32[32,128]{1,0:T(8,128)}, f32[32,128]{1,0:T(8,128)S(1)}, u32[]{:S(2)}) copy-start(f32[32,128]{1,0:T(8,128)S(1)} %collective-permute-done.5.chip_ref) | copy-start | bytes 49156
  20.7 1.2 %collective-permute-start.6 = (f32[16,128]{1,0:T(8,128)S(1)}, f32[16,128]{1,0:T(8,128)S(1)}, u32[]{:S(2)}, u32[]{:S(2)}) collective-permute-start(f32[16,128]{1,0:T(8,128)S(1)} %slice.4), channel_id=1, source_target_pairs={{0,1},{1,0},{2,3},{3,2},{4,5},{5,4},{6,7},{7,6},{8,9},{9,8},{10,11... | collective-permute-start | bytes 24584 | tf_op jit(solution)/shard_map/ppermute | solution.py:32
  20.9 1.0 %copy-start.5 = (f32[16,128]{1,0:T(8,128)}, f32[16,128]{1,0:T(8,128)S(1)}, u32[]{:S(2)}) copy-start(f32[16,128]{1,0:T(8,128)S(1)} %collective-permute-done.4.core_ref) | copy-start | bytes 24580
  21.9 0.6 %copy-start.6 = (f32[16,128]{1,0:T(8,128)}, f32[16,128]{1,0:T(8,128)S(1)}, u32[]{:S(2)}) copy-start(f32[16,128]{1,0:T(8,128)S(1)} %collective-permute-done.6.relay_ref) | copy-start | bytes 24580

commit v2 on v1

--- a/solution.py
+++ b/solution.py
@@ -1,4 +1,5 @@
 import functools
+import math
 
 import jax
 import jax.numpy as jnp
@@ -13,7 +14,7 @@
 GROUP = ("tile", "depth", "sub")
 NT = (((1,), (1,)), ((), ()))
 VMEM = pl.BlockSpec(memory_space=pltpu.VMEM)
-SMEM = pl.BlockSpec(memory_space=pltpu.SMEM)
+HBM = pl.BlockSpec(memory_space=pltpu.HBM)
 
 
 def parity(number):
@@ -40,10 +41,23 @@
     return lax.axis_index("depth") * sub_count + lax.axis_index("sub")
 
 
-def prepare_kernel(
-    dims, left_ref, left_exp_ref, right_ref, right_exp_ref, mask_ref, block_ref, left_out, right_out, left_f32
-):
+def prepare_kernel(dims, *refs):
     channels, _, sub_count = dims
+    params = (len(refs) - 15) // 2
+    sources, refs = refs[: 5 + params], refs[5 + params :]
+    block_ref, left_out, right_out = refs[:3]
+    params_out, refs = refs[3 : 3 + params], refs[3 + params :]
+    left_ref, left_exp_ref, right_ref, right_exp_ref, mask_ref, left_f32, semaphores = refs
+    copies = [
+        pltpu.make_async_copy(source, target, semaphores.at[n])
+        for n, (source, target) in enumerate(
+            zip(sources, (left_ref, left_exp_ref, right_ref, right_exp_ref, mask_ref, *params_out))
+        )
+    ]
+    for copy in copies:
+        copy.start()
+    for copy in copies[:5]:
+        copy.wait()
     band = left_exp_ref.shape[0]
     piece = right_exp_ref.shape[0]
     fold = channels // ROWS
@@ -77,6 +91,8 @@
     for i in range(band):
         at = pl.multiple_of((mine ^ i) * channels, channels)
         left_out[i * channels : (i + 1) * channels, :] = left_f32[pl.ds(at, channels), :].astype(jnp.bfloat16)
+    for copy in copies[5:]:
+        copy.wait()
 
 
 def spread_kernel(
@@ -227,8 +243,19 @@
                 bins_out[:, pl.ds(at, LANES)] = line
 
 
-def cost(flops, size):
-    return pl.CostEstimate(flops=flops, bytes_accessed=size, transcendentals=0)
+def call(kernel, flops, outs, scratch, operands, place=VMEM):
+    arrays = [(a.shape, a.dtype) for a in (*operands, *outs)]
+    arrays += [(a.shape, a.dtype) for a in scratch if a.memory_space == pltpu.VMEM]
+    size = sum(math.prod(dims) * jnp.dtype(kind).itemsize for dims, kind in arrays)
+    return pl.pallas_call(
+        kernel,
+        out_shape=outs,
+        in_specs=[place] * len(operands),
+        out_specs=(VMEM,) * len(outs),
+        scratch_shapes=scratch,
+        compiler_params=pltpu.CompilerParams(vmem_limit_bytes=min(2 * size + (2 << 20), 60 << 20)),
+        cost_estimate=pl.CostEstimate(flops=flops, bytes_accessed=size, transcendentals=0),
+    )(*(pltpu.with_memory_space_constraint(a, pltpu.HBM) if place is HBM else a for a in operands))
 
 
 def shape(rows, columns, kind):
@@ -263,52 +290,64 @@
     dims = (channels, depth_count, sub_count)
     bf16, f32 = jnp.bfloat16, jnp.float32
 
-    own, left_rows, right_rows = pl.pallas_call(
+    sources = (left_mantissa, left_exponent.T, right_mantissa.T, right_exponent.T, residue_mask)
+    params = (
+        out_weight,
+        out_bias.reshape(1, -1),
+        gate_weight,
+        up_weight,
+        down_weight,
+        distogram_weight.T,
+        distogram_bias.reshape(1, -1),
+    )
+    own, left_rows, right_rows, *params = call(
         functools.partial(prepare_kernel, dims),
-        out_shape=(
+        1 << 16,
+        (
             shape(2 * piece * channels, seqs, bf16),
             shape(band * channels, seqs, bf16),
             shape(piece * channels, seqs, bf16),
+            *(shape(*p.shape, p.dtype) for p in params),
         ),
-        in_specs=[VMEM] * 4 + [SMEM],
-        out_specs=(VMEM,) * 3,
-        scratch_shapes=[pltpu.VMEM((band * channels, seqs), f32)],
-        cost_estimate=cost(1 << 16, 1 << 17),
-        name="prepare",
-    )(left_mantissa, left_exponent.T, right_mantissa.T, right_exponent.T, residue_mask)
+        [pltpu.VMEM(s.shape, s.dtype) for s in sources[:4]]
+        + [
+            pltpu.SMEM(residue_mask.shape, residue_mask.dtype),
+            pltpu.VMEM((band * channels, seqs), f32),
+            pltpu.SemaphoreType.DMA((len(sources) + len(params),)),
+        ],
+        (*sources, *params),
+        HBM,
+    )
+    out_weight = params[0]
     blocks = {0: own}
     for bit in bits_of(tile_count):
         for bits in list(blocks):
             blocks[bits ^ bit] = xor_permute(blocks[bits], bit, 0, 1)
     other_rows = xor_permute(right_rows, 0, 0, 1)
-    left_spread, right_spread, swapped = pl.pallas_call(
+    left_spread, right_spread, swapped = call(
         functools.partial(spread_kernel, dims),
-        out_shape=(
+        1 << 16,
+        (
             shape(band * fold * channels, fold * seqs, bf16),
             shape(band * fold * channels, fold * seqs, bf16),
             shape(*out_weight.shape, bf16),
         ),
-        in_specs=[VMEM] * 4,
-        out_specs=(VMEM,) * 3,
-        scratch_shapes=[pltpu.VMEM((sub_count, piece, channels, seqs), bf16), pltpu.VMEM(out_weight.shape, f32)],
-        cost_estimate=cost(1 << 16, 1 << 20),
-        name="spread",
-    )(left_rows, right_rows, other_rows, out_weight)
+        [pltpu.VMEM((sub_count, piece, channels, seqs), bf16), pltpu.VMEM(out_weight.shape, f32)],
+        (left_rows, right_rows, other_rows, out_weight),
+    )
     block_tiles = tuple(sorted(blocks))
     count = len(block_tiles) * piece
-    keep, core, chip = pl.pallas_call(
+    keep, core, chip = call(
         functools.partial(pair_kernel, dims, len(block_tiles)),
-        out_shape=(
+        1 << 27,
+        (
             shape(2 * count, pair_channels, f32),
             shape(2 * count, pair_channels, f32),
             shape(max(band - sub_count, 1) * 2 * count, pair_channels, f32),
         ),
-        in_specs=[VMEM] * (len(block_tiles) + 4),
-        out_specs=(VMEM,) * 3,
-        scratch_shapes=[pltpu.VMEM((2 * band, count * ROWS, fold * channels), f32)],
-        cost_estimate=cost(1 << 27, 1 << 21),
-        name="pair",
-    )(*(blocks[k] for k in block_tiles), left_spread, right_spread, out_weight, swapped)
+        [pltpu.VMEM((2 * band, count * ROWS, fold * channels), f32)],
+        (*(blocks[k] for k in block_tiles), left_spread, right_spread, out_weight, swapped),
+    )
     size = sub_count * 2 * count
     for bit in bits_of(depth_count)[:-1]:
         rows = jnp.concatenate([keep, core, chip], axis=0)
@@ -319,24 +358,18 @@
     from_chip = xor_permute(chip, 0, 1, 1) if depth_count > 1 else chip
     from_core = xor_permute(core, 0, 0, 1)
     relayed = xor_permute(from_chip[: 2 * count], 0, 0, 1) if depth_count > 1 else from_core
-    return pl.pallas_call(
+    return call(
         functools.partial(finish_kernel, dims, block_tiles, seqs * depth_count),
-        out_shape=(shape(1, residues * pair_channels, bf16), shape(1, residues * bins, f32)),
-        in_specs=[VMEM] * 10,
-        out_specs=(VMEM, VMEM),
-        cost_estimate=cost(1 << 25, 1 << 20),
-        name="finish",
-    )(
-        keep,
-        from_core,
-        from_chip,
-        relayed,
-        out_bias.reshape(1, -1),
-        gate_weight,
-        up_weight,
-        down_weight,
-        distogram_weight.T,
-        distogram_bias.reshape(1, -1),
+        1 << 25,
+        (shape(1, residues * pair_channels, bf16), shape(1, residues * bins, f32)),
+        [],
+        (
+            keep,
+            from_core,
+            from_chip,
+            relayed,
+            *params[1:],
+        ),
     )
 
 

time: 25 us -> 17.5 us (0.70)
  Pallas kernels: 8.85 us -> 3.7 us
  local copies, waits for them, and re-layouts: 1.8 us -> 0.01 us
  waiting for transfers between devices: 4.15 us -> 3.25 us
  starting transfers between devices: 9.31 us -> 9.71 us
    pallas_call x4, Pallas kernels: 8.85 us -> 3.7 us  [call(): pl.pallas_call(kernel, out_shape=outs, in_specs=[place] * len(operands),...]
    unnamed x14 -> x0, local copies, waits for them, and re-layouts: 1.79 us -> none
    ppermute x7, waiting for transfers between devices: 4.15 us -> 3.25 us  [xor_permute(): return lax.ppermute(value, GROUP, pairs)]
    ppermute x7, starting transfers between devices: 9.31 us -> 9.71 us  [xor_permute(): return lax.ppermute(value, GROUP, pairs)]
  transfers between devices with their start and end apart: 7 -> 7, of which waited for: 4 -> 3; matrix products, arithmetic and copies ran while one was open for 0% -> 0% of each run, Pallas kernels for 9% -> 2%
where the time goes in v2:
time: 17.5 us; the launch traced here: 17.3 us
  starting transfers between devices  9.71 us (55%)
  Pallas kernels  3.7 us (21%)
  waiting for transfers between devices  3.25 us (19%)
  between operations  0.67 us (4%)
    ppermute x7, starting transfers between devices, xor_permute(): return lax.ppermute(value, GROUP, pairs)  9.71 us
    pallas_call x4, Pallas kernels, call(): pl.pallas_call(kernel, out_shape=outs, in_specs=[place] * len(operands),...  3.7 us
    ppermute x7, waiting for transfers between devices, xor_permute(): return lax.ppermute(value, GROUP, pairs)  3.25 us
  transfers between devices with their start and end apart: 7, of which 3 were waited for; matrix products, arithmetic and copies ran while one was open for 0% of the time, Pallas kernels for 2%

profile of v2, /device:TPU:0, one launch (start us, length us, event | category | flops | bytes accessed | tf_op | source)
XLA Modules:
  0.0 17.3 jit_solution(3953274388107731242)
XLA Ops:
  0.6 1.3 %shard_map.131 = (bf16[128,128]{1,0:T(8,128)(2,1)S(1)}, bf16[128,128]{1,0:T(8,128)(2,1)S(1)}, bf16[64,128]{1,0:T(8,128)(2,1)S(1)}, bf16[1024,128]{1,0:T(8,128)(2...) custom-call(bf16[128,128]{1,0:T(8,128)(2,1)} %refs_0_.1, ...), custom_call_target="tpu_custom_call" | custom-call | flops 65536 | bytes 1596992 | tf_op jit(solution)/shard_map/pallas_call | solution.py:250
  2.0 3.6 %collective-permute-start.1 = (bf16[128,128]{1,0:T(8,128)(2,1)S(1)}, bf16[128,128]{1,0:T(8,128)(2,1)S(1)}, u32[]{:S(2)}, u32[]{:S(2)}) collective-permute-start(bf16[128,128]{1,0:T(8,128)(2,1)S(1)} %get-tuple-element.18.refs_0_), channel_id=1, source_target_pairs={{0,9},{1,8},{2,11},{3,10},{4,13},{5,12},{6,15},{7,14},{8,1},{9,0},... | collective-permute-start | bytes 98312 | tf_op jit(solution)/shard_map/ppermute | solution.py:33
  5.5 1.9 %collective-permute-start = (bf16[128,128]{1,0:T(8,128)(2,1)S(1)}, bf16[128,128]{1,0:T(8,128)(2,1)S(1)}, u32[]{:S(2)}, u32[]{:S(2)}) collective-permute-start(bf16[128,128]{1,0:T(8,128)(2,1)S(1)} %get-tuple-element.18.refs_0_), channel_id=1, source_target_pairs={{0,5},{1,4},{2,7},{3,6},{4,1},{5,0},{6,3},{7,2},{8,13},{9,12},{10,... | collective-permute-start | bytes 98312 | tf_op jit(solution)/shard_map/ppermute | solution.py:33
  7.4 0.0 collective-permute-done.1.refs_2_
  7.4 1.9 %collective-permute-start.2 = (bf16[128,128]{1,0:T(8,128)(2,1)S(1)}, bf16[128,128]{1,0:T(8,128)(2,1)S(1)}, u32[]{:S(2)}, u32[]{:S(2)}) collective-permute-start(bf16[128,128]{1,0:T(8,128)(2,1)S(1)} %collective-permute-done.1.refs_2_), channel_id=1, source_target_pairs={{0,5},{1,4},{2,7},{3,6},{4,1},{5,0},{6,3},{7,2},{8,13},{9,12},{10,... | collective-permute-start | bytes 98312 | tf_op jit(solution)/shard_map/ppermute | solution.py:33
  9.3 0.2 %collective-permute-start.3 = (bf16[64,128]{1,0:T(8,128)(2,1)S(1)}, bf16[64,128]{1,0:T(8,128)(2,1)S(1)}, u32[]{:S(2)}, u32[]{:S(2)}) collective-permute-start(bf16[64,128]{1,0:T(8,128)(2,1)S(1)} %get-tuple-element.20.right_ref), channel_id=1, source_target_pairs={{0,1},{1,0},{2,3},{3,2},{4,5},{5,4},{6,7},{7,6},{8,9},{9,8},{10,11... | collective-permute-start | bytes 49160 | tf_op jit(solution)/shard_map/ppermute | solution.py:33
  9.5 1.0 %collective-permute-done.3.other_ref = bf16[64,128]{1,0:T(8,128)(2,1)S(1)} collective-permute-done((bf16[64,128]{1,0:T(8,128)(2,1)S(1)}, bf16[64,128]{1,0:T(8,128)(2,1)S(1)}, u32[]{:S(2)}, u32[]{:S(2)}) %collective-permute-start.3) | collective-permute-done | bytes 16416 | tf_op jit(solution)/shard_map/ppermute | solution.py:33
  10.5 0.4 %shard_map.132 = (bf16[512,512]{1,0:T(8,128)(2,1)S(1)}, bf16[512,512]{1,0:T(8,128)(2,1)S(1)}, bf16[1024,128]{1,0:T(8,128)(2,1)S(1)}) custom-call(bf16[128,128]{1,0:T(8,128)(2,1)S(1)} %get-tuple-element.19.left_ref, bf16[64,128]{1,0:T(8,128)(2,1)S(1)} %get-tuple-element.20.right_ref, bf16[64,128]{1,0:T(8,128)(2,1)S(1)} %collective-permute-done.3.other_ref, ...), custom_call_target="tpu_custom_call" | custom-call | flops 65536 | bytes 2195456 | tf_op jit(solution)/shard_map/pallas_call | solution.py:250
  10.9 0.0 collective-permute-done.refs_1_
  10.9 0.0 collective-permute-done.2.refs_3_
  11.0 0.8 %shard_map.133 = (f32[16,128]{1,0:T(8,128)S(1)}, f32[16,128]{1,0:T(8,128)S(1)}, f32[32,128]{1,0:T(8,128)S(1)}) custom-call(bf16[128,128]{1,0:T(8,128)(2,1)S(1)} %get-tuple-element.18.refs_0_, bf16[128,128]{1,0:T(8,128)(2,1)S(1)} %collective-permute-done.refs_1_, bf16[128,128]{1,0:T(8,128)(2,1)S(1)} %collective-permute-done.1.refs_2_, ...), custom_call_target="tpu_custom_call" | custom-call | flops 134217728 | bytes 1998848 | tf_op jit(solution)/shard_map/pallas_call | solution.py:250
  11.8 1.5 %collective-permute-start.5 = (f32[32,128]{1,0:T(8,128)S(1)}, f32[32,128]{1,0:T(8,128)S(1)}, u32[]{:S(2)}, u32[]{:S(2)}) collective-permute-start(f32[32,128]{1,0:T(8,128)S(1)} %get-tuple-element.27), channel_id=1, source_target_pairs={{0,3},{1,2},{2,1},{3,0},{4,7},{5,6},{6,5},{7,4},{8,11},{9,10},{10,... | collective-permute-start | bytes 49160 | tf_op jit(solution)/shard_map/ppermute | solution.py:33
  13.3 0.4 %collective-permute-start.4 = (f32[16,128]{1,0:T(8,128)S(1)}, f32[16,128]{1,0:T(8,128)S(1)}, u32[]{:S(2)}, u32[]{:S(2)}) collective-permute-start(f32[16,128]{1,0:T(8,128)S(1)} %get-tuple-element.26), channel_id=1, source_target_pairs={{0,1},{1,0},{2,3},{3,2},{4,5},{5,4},{6,7},{7,6},{8,9},{9,8},{10,11... | collective-permute-start | bytes 24584 | tf_op jit(solution)/shard_map/ppermute | solution.py:33
  13.7 1.3 %collective-permute-done.5.chip_ref = f32[32,128]{1,0:T(8,128)S(1)} collective-permute-done((f32[32,128]{1,0:T(8,128)S(1)}, f32[32,128]{1,0:T(8,128)S(1)}, u32[]{:S(2)}, u32[]{:S(2)}) %collective-permute-start.5) | collective-permute-done | bytes 16416 | tf_op jit(solution)/shard_map/ppermute | solution.py:33
  15.0 0.2 %collective-permute-start.6 = (f32[16,128]{1,0:T(8,128)S(1)}, f32[16,128]{1,0:T(8,128)S(1)}, u32[]{:S(2)}, u32[]{:S(2)}) collective-permute-start(f32[16,128]{1,0:T(8,128)S(1)} %slice.4), channel_id=1, source_target_pairs={{0,1},{1,0},{2,3},{3,2},{4,5},{5,4},{6,7},{7,6},{8,9},{9,8},{10,11... | collective-permute-start | bytes 24584 | tf_op jit(solution)/shard_map/ppermute | solution.py:33
  15.2 0.0 collective-permute-done.4.core_ref
  15.2 1.0 %collective-permute-done.6.relay_ref = f32[16,128]{1,0:T(8,128)S(1)} collective-permute-done((f32[16,128]{1,0:T(8,128)S(1)}, f32[16,128]{1,0:T(8,128)S(1)}, u32[]{:S(2)}, u32[]{:S(2)}) %collective-permute-start.6) | collective-permute-done | bytes 8224 | tf_op jit(solution)/shard_map/ppermute | solution.py:33
  16.2 1.2 %shard_map.134 = (bf16[1,2048]{1,0:T(2,128)(2,1)}, f32[1,1024]{1,0:T(1,128)}) custom-call(f32[16,128]{1,0:T(8,128)S(1)} %get-tuple-element.25.keep_ref, f32[16,128]{1,0:T(8,128)S(1)} %collective-permute-done.4.core_ref, f32[32,128]{1,0:T(8,128)S(1)} %collective-permute-done.5.chip_ref, f32[16,128]{1,0:T(8,128)S(1)} %collective-permute-done.6.relay_ref, ...), custom_call_target="tpu_custom_call" | custom-call | flops 33554432 | bytes 459520 | tf_op jit(solution)/shard_map/pallas_call | solution.py:250
  (1 shorter events, 0.0 us)
Async XLA Ops:
  2.0 5.4 %collective-permute-start.1 = (bf16[128,128]{1,0:T(8,128)(2,1)S(1)}, bf16[128,128]{1,0:T(8,128)(2,1)S(1)}, u32[]{:S(2)}, u32[]{:S(2)}) collective-permute-start(bf16[128,128]{1,0:T(8,128)(2,1)S(1)} %get-tuple-element.18.refs_0_), channel_id=1, source_target_pairs={{0,9},{1,8},{2,11},{3,10},{4,13},{5,12},{6,15},{7,14},{8,1},{9,0},... | collective-permute-start | bytes 98312 | tf_op jit(solution)/shard_map/ppermute | solution.py:33
  5.5 5.4 %collective-permute-start = (bf16[128,128]{1,0:T(8,128)(2,1)S(1)}, bf16[128,128]{1,0:T(8,128)(2,1)S(1)}, u32[]{:S(2)}, u32[]{:S(2)}) collective-permute-start(bf16[128,128]{1,0:T(8,128)(2,1)S(1)} %get-tuple-element.18.refs_0_), channel_id=1, source_target_pairs={{0,5},{1,4},{2,7},{3,6},{4,1},{5,0},{6,3},{7,2},{8,13},{9,12},{10,... | collective-permute-start | bytes 98312 | tf_op jit(solution)/shard_map/ppermute | solution.py:33
  7.4 3.6 %collective-permute-start.2 = (bf16[128,128]{1,0:T(8,128)(2,1)S(1)}, bf16[128,128]{1,0:T(8,128)(2,1)S(1)}, u32[]{:S(2)}, u32[]{:S(2)}) collective-permute-start(bf16[128,128]{1,0:T(8,128)(2,1)S(1)} %collective-permute-done.1.refs_2_), channel_id=1, source_target_pairs={{0,5},{1,4},{2,7},{3,6},{4,1},{5,0},{6,3},{7,2},{8,13},{9,12},{10,... | collective-permute-start | bytes 98312 | tf_op jit(solution)/shard_map/ppermute | solution.py:33
  9.3 1.2 %collective-permute-start.3 = (bf16[64,128]{1,0:T(8,128)(2,1)S(1)}, bf16[64,128]{1,0:T(8,128)(2,1)S(1)}, u32[]{:S(2)}, u32[]{:S(2)}) collective-permute-start(bf16[64,128]{1,0:T(8,128)(2,1)S(1)} %get-tuple-element.20.right_ref), channel_id=1, source_target_pairs={{0,1},{1,0},{2,3},{3,2},{4,5},{5,4},{6,7},{7,6},{8,9},{9,8},{10,11... | collective-permute-start | bytes 49160 | tf_op jit(solution)/shard_map/ppermute | solution.py:33
  11.8 3.2 %collective-permute-start.5 = (f32[32,128]{1,0:T(8,128)S(1)}, f32[32,128]{1,0:T(8,128)S(1)}, u32[]{:S(2)}, u32[]{:S(2)}) collective-permute-start(f32[32,128]{1,0:T(8,128)S(1)} %get-tuple-element.27), channel_id=1, source_target_pairs={{0,3},{1,2},{2,1},{3,0},{4,7},{5,6},{6,5},{7,4},{8,11},{9,10},{10,... | collective-permute-start | bytes 49160 | tf_op jit(solution)/shard_map/ppermute | solution.py:33
  13.3 1.9 %collective-permute-start.4 = (f32[16,128]{1,0:T(8,128)S(1)}, f32[16,128]{1,0:T(8,128)S(1)}, u32[]{:S(2)}, u32[]{:S(2)}) collective-permute-start(f32[16,128]{1,0:T(8,128)S(1)} %get-tuple-element.26), channel_id=1, source_target_pairs={{0,1},{1,0},{2,3},{3,2},{4,5},{5,4},{6,7},{7,6},{8,9},{9,8},{10,11... | collective-permute-start | bytes 24584 | tf_op jit(solution)/shard_map/ppermute | solution.py:33
  15.0 1.2 %collective-permute-start.6 = (f32[16,128]{1,0:T(8,128)S(1)}, f32[16,128]{1,0:T(8,128)S(1)}, u32[]{:S(2)}, u32[]{:S(2)}) collective-permute-start(f32[16,128]{1,0:T(8,128)S(1)} %slice.4), channel_id=1, source_target_pairs={{0,1},{1,0},{2,3},{3,2},{4,5},{5,4},{6,7},{7,6},{8,9},{9,8},{10,11... | collective-permute-start | bytes 24584 | tf_op jit(solution)/shard_map/ppermute | solution.py:33

commit v3 on v2

--- a/solution.py
+++ b/solution.py
@@ -41,22 +41,21 @@
     return lax.axis_index("depth") * sub_count + lax.axis_index("sub")
 
 
-def prepare_kernel(dims, *refs):
-    channels, _, sub_count = dims
-    params = (len(refs) - 15) // 2
-    sources, refs = refs[: 5 + params], refs[5 + params :]
-    block_ref, left_out, right_out = refs[:3]
-    params_out, refs = refs[3 : 3 + params], refs[3 + params :]
-    left_ref, left_exp_ref, right_ref, right_exp_ref, mask_ref, left_f32, semaphores = refs
+def fetch(sources, targets, semaphores):
     copies = [
         pltpu.make_async_copy(source, target, semaphores.at[n])
-        for n, (source, target) in enumerate(
-            zip(sources, (left_ref, left_exp_ref, right_ref, right_exp_ref, mask_ref, *params_out))
-        )
+        for n, (source, target) in enumerate(zip(sources, targets))
     ]
     for copy in copies:
         copy.start()
-    for copy in copies[:5]:
+    return copies
+
+
+def prepare_kernel(dims, *refs):
+    channels, _, sub_count = dims
+    sources, (block_ref, left_out, right_out), scratch = refs[:5], refs[5:8], refs[8:]
+    left_ref, left_exp_ref, right_ref, right_exp_ref, mask_ref, left_f32, semaphores = scratch
+    for copy in fetch(sources, scratch, semaphores):
         copy.wait()
     band = left_exp_ref.shape[0]
     piece = right_exp_ref.shape[0]
@@ -91,51 +90,71 @@
     for i in range(band):
         at = pl.multiple_of((mine ^ i) * channels, channels)
         left_out[i * channels : (i + 1) * channels, :] = left_f32[pl.ds(at, channels), :].astype(jnp.bfloat16)
-    for copy in copies[5:]:
-        copy.wait()
-
-
-def spread_kernel(
-    dims, left_ref, right_ref, other_ref, weight_ref, left_spread, right_spread, weight_out, both, weight_f32
-):
+
+
+def arrange_kernel(dims, *refs):
     channels, _, sub_count = dims
-    seqs = left_ref.shape[1]
-    band = left_ref.shape[0] // channels
+    params = (len(refs) - 7) // 2
+    right_ref, other_ref = refs[:2]
+    sources, refs = refs[2 : 2 + params], refs[2 + params :]
+    right_out, swapped_out = refs[:2]
+    targets, (both, weight_f32, semaphores) = refs[2 : 2 + params], refs[2 + params :]
+    copies = fetch(sources, targets, semaphores)
+    seqs = right_ref.shape[1]
     piece = right_ref.shape[0] // channels
     fold = channels // ROWS
     sub = lax.axis_index("sub")
     mine = row_in_tile(sub_count)
     both[sub] = right_ref[...].reshape(piece, channels, seqs)
     both[1 - sub] = other_ref[...].reshape(piece, channels, seqs)
-    left_spread[...] = jnp.zeros_like(left_spread)
-    right_spread[...] = jnp.zeros_like(right_spread)
-    for i in range(band):
+    for i in range(right_out.shape[0] // channels):
         here = mine ^ i
-        left = left_ref[i * channels : (i + 1) * channels, :]
-        right = both[here // piece, here % piece]
-        for x in range(fold):
-            at = (i * fold + x) * channels
-            left_spread[at : at + channels, x * seqs : (x + 1) * seqs] = left
-            right_spread[at : at + channels, x * seqs : (x + 1) * seqs] = right
-    weight_f32[...] = weight_ref[...].astype(jnp.float32)
+        right_out[i * channels : (i + 1) * channels, :] = both[here // piece, here % piece]
+    copies[0].wait()
+    weight_f32[...] = targets[0][...].astype(jnp.float32)
     for g in range(ROWS):
         for x in range(fold):
             at = (g * fold + x) * channels
             rows = weight_f32[pl.ds(x * ROWS + g, channels, stride=channels), :]
-            weight_out[at : at + channels, :] = rows.astype(jnp.bfloat16)
+            swapped_out[at : at + channels, :] = rows.astype(jnp.bfloat16)
+    for copy in copies[1:]:
+        copy.wait()
+
+
+def trade_chunks(arrays, width):
+    chunk = lax.broadcasted_iota(jnp.int32, arrays[0].shape, 1) // width
+    for bit in bits_of(len(arrays)):
+        keep = (chunk & bit) == 0
+        for x in range(len(arrays)):
+            if x & bit:
+                continue
+            low, high = arrays[x], arrays[x | bit]
+            arrays[x] = jnp.where(keep, low, pltpu.roll(high, bit * width, 1))
+            arrays[x | bit] = jnp.where(keep, pltpu.roll(low, LANES - bit * width, 1), high)
+    return arrays
 
 
 def pair_kernel(dims, block_count, *refs):
     channels, _, sub_count = dims
     blocks = refs[:block_count]
-    left_spread, right_spread, weight_ref, swapped_ref, keep_ref, core_ref, chip_ref, outer = refs[block_count:]
+    left_ref, right_ref, weight_ref, swapped_ref, keep_ref, core_ref, chip_ref, outer = refs[block_count:]
     fold = channels // ROWS
     half = blocks[0].shape[0] // 2
     size = half // fold
-    piece = size // ROWS
-    count = block_count * piece
-    band = left_spread.shape[0] // (fold * channels)
-    width = fold * channels
+    count = block_count * size // ROWS
+    rows = count * ROWS
+    band = left_ref.shape[0] // channels
+    for way, own in enumerate((left_ref, right_ref)):
+        base = half * (1 - way)
+        factor = jnp.concatenate(
+            [b[base + x * size : base + (x + 1) * size, :] for x in range(fold) for b in blocks], axis=0
+        )
+        product = lax.dot_general(factor, own[...], NT, preferred_element_type=jnp.float32)
+        for i in range(0, band, fold):
+            lanes = slice(i * channels, i * channels + LANES)
+            parts = [product[x * rows : (x + 1) * rows, lanes] for x in range(fold)]
+            for n, part in enumerate(trade_chunks(parts, channels)):
+                outer[way * band + i + n] = part
     natural = jnp.concatenate(
         [
             weight_ref[(x * ROWS + g) * channels : (x * ROWS + g + 1) * channels, :]
@@ -144,19 +163,7 @@
         ],
         axis=0,
     )
-    for way in range(2):
-        base = half * (1 - way)
-        factor = jnp.concatenate(
-            [
-                jnp.concatenate([b[base + x * size : base + (x + 1) * size, :] for b in blocks], axis=0)
-                for x in range(fold)
-            ],
-            axis=1,
-        )
-        spread = left_spread if way == 0 else right_spread
-        product = lax.dot_general(factor, spread[...], NT, preferred_element_type=jnp.float32)
-        for i in range(band):
-            outer[way * band + i] = product[:, i * width : (i + 1) * width]
+    for way, weight in enumerate((swapped_ref[...], natural)):
         flat = jnp.concatenate(
             [
                 jnp.concatenate(
@@ -169,7 +176,6 @@
         )
         high = flat.astype(jnp.bfloat16)
         low = (flat - high.astype(jnp.float32)).astype(jnp.bfloat16)
-        weight = swapped_ref[...] if way == 0 else natural
         terms = jnp.dot(jnp.concatenate([high, low], axis=0), weight, preferred_element_type=jnp.float32)
         terms = terms[: band * count] + terms[band * count :]
         place = lambda i: slice(i * count, (i + 1) * count)
@@ -243,19 +249,19 @@
                 bins_out[:, pl.ds(at, LANES)] = line
 
 
-def call(kernel, flops, outs, scratch, operands, place=VMEM):
+def call(kernel, flops, outs, scratch, operands, sources=()):
     arrays = [(a.shape, a.dtype) for a in (*operands, *outs)]
     arrays += [(a.shape, a.dtype) for a in scratch if a.memory_space == pltpu.VMEM]
     size = sum(math.prod(dims) * jnp.dtype(kind).itemsize for dims, kind in arrays)
     return pl.pallas_call(
         kernel,
         out_shape=outs,
-        in_specs=[place] * len(operands),
+        in_specs=[VMEM] * len(operands) + [HBM] * len(sources),
         out_specs=(VMEM,) * len(outs),
         scratch_shapes=scratch,
         compiler_params=pltpu.CompilerParams(vmem_limit_bytes=min(2 * size + (2 << 20), 60 << 20)),
         cost_estimate=pl.CostEstimate(flops=flops, bytes_accessed=size, transcendentals=0),
-    )(*(pltpu.with_memory_space_constraint(a, pltpu.HBM) if place is HBM else a for a in operands))
+    )(*operands, *(pltpu.with_memory_space_constraint(s, pltpu.HBM) for s in sources))
 
 
 def shape(rows, columns, kind):
@@ -285,12 +291,34 @@
     residues = residue_mask.shape[0]
     pair_channels = out_weight.shape[1]
     bins = distogram_weight.shape[1]
-    if sub_count != 2 or band != depth_count * sub_count or tile_count & (tile_count - 1) or band & (band - 1):
+    if channels * fold != LANES or band % fold or sub_count != 2 or band != depth_count * sub_count or tile_count & (tile_count - 1) or band & (band - 1):
         raise ValueError("unsupported mesh")
     dims = (channels, depth_count, sub_count)
     bf16, f32 = jnp.bfloat16, jnp.float32
 
     sources = (left_mantissa, left_exponent.T, right_mantissa.T, right_exponent.T, residue_mask)
+    own, left_rows, right_rows = call(
+        functools.partial(prepare_kernel, dims),
+        1 << 16,
+        (
+            shape(2 * piece * channels, seqs, bf16),
+            shape(band * channels, seqs, bf16),
+            shape(piece * channels, seqs, bf16),
+        ),
+        [pltpu.VMEM(s.shape, s.dtype) for s in sources[:4]]
+        + [
+            pltpu.SMEM(residue_mask.shape, residue_mask.dtype),
+            pltpu.VMEM((band * channels, seqs), f32),
+            pltpu.SemaphoreType.DMA((len(sources),)),
+        ],
+        (),
+        sources,
+    )
+    blocks = {0: own}
+    for bit in bits_of(tile_count):
+        for bits in list(blocks):
+            blocks[bits ^ bit] = xor_permute(blocks[bits], bit, 0, 1)
+    other_rows = xor_permute(right_rows, 0, 0, 1)
     params = (
         out_weight,
         out_bias.reshape(1, -1),
@@ -300,40 +328,21 @@
         distogram_weight.T,
         distogram_bias.reshape(1, -1),
     )
-    own, left_rows, right_rows, *params = call(
-        functools.partial(prepare_kernel, dims),
+    right_rows, swapped, weight, *params = call(
+        functools.partial(arrange_kernel, dims),
         1 << 16,
         (
-            shape(2 * piece * channels, seqs, bf16),
             shape(band * channels, seqs, bf16),
-            shape(piece * channels, seqs, bf16),
+            shape(*out_weight.shape, bf16),
             *(shape(*p.shape, p.dtype) for p in params),
         ),
-        [pltpu.VMEM(s.shape, s.dtype) for s in sources[:4]]
-        + [
-            pltpu.SMEM(residue_mask.shape, residue_mask.dtype),
-            pltpu.VMEM((band * channels, seqs), f32),
-            pltpu.SemaphoreType.DMA((len(sources) + len(params),)),
+        [
+            pltpu.VMEM((sub_count, piece, channels, seqs), bf16),
+            pltpu.VMEM(out_weight.shape, f32),
+            pltpu.SemaphoreType.DMA((len(params),)),
         ],
-        (*sources, *params),
-        HBM,
-    )
-    out_weight = params[0]
-    blocks = {0: own}
-    for bit in bits_of(tile_count):
-        for bits in list(blocks):
-            blocks[bits ^ bit] = xor_permute(blocks[bits], bit, 0, 1)
-    other_rows = xor_permute(right_rows, 0, 0, 1)
-    left_spread, right_spread, swapped = call(
-        functools.partial(spread_kernel, dims),
-        1 << 16,
-        (
-            shape(band * fold * channels, fold * seqs, bf16),
-            shape(band * fold * channels, fold * seqs, bf16),
-            shape(*out_weight.shape, bf16),
-        ),
-        [pltpu.VMEM((sub_count, piece, channels, seqs), bf16), pltpu.VMEM(out_weight.shape, f32)],
-        (left_rows, right_rows, other_rows, out_weight),
+        (right_rows, other_rows),
+        params,
     )
     block_tiles = tuple(sorted(blocks))
     count = len(block_tiles) * piece
@@ -345,8 +354,8 @@
             shape(2 * count, pair_channels, f32),
             shape(max(band - sub_count, 1) * 2 * count, pair_channels, f32),
         ),
-        [pltpu.VMEM((2 * band, count * ROWS, fold * channels), f32)],
-        (*(blocks[k] for k in block_tiles), left_spread, right_spread, out_weight, swapped),
+        [pltpu.VMEM((2 * band, count * ROWS, LANES), f32)],
+        (*(blocks[k] for k in block_tiles), left_rows, right_rows, weight, swapped),
     )
     size = sub_count * 2 * count
     for bit in bits_of(depth_count)[:-1]:
@@ -368,7 +377,7 @@
             from_core,
             from_chip,
             relayed,
-            *params[1:],
+            *params,
         ),
     )
 

time: 17.5 us -> 17.9 us (1.023)
  Pallas kernels: 3.7 us -> 4.06 us
  waiting for transfers between devices: 3.25 us -> 3.52 us
  starting transfers between devices: 9.71 us -> 9.45 us
    pallas_call x4, Pallas kernels: 3.7 us -> 4.06 us  [call(): pl.pallas_call(kernel, out_shape=outs, in_specs=[VMEM] * len(operands) +...]
    ppermute x7, starting transfers between devices: 9.71 us -> 9.45 us  [xor_permute(): return lax.ppermute(value, GROUP, pairs)]
    ppermute x7, waiting for transfers between devices: 3.25 us -> 3.52 us  [xor_permute(): return lax.ppermute(value, GROUP, pairs)]
  transfers between devices with their start and end apart: 7 -> 7, of which waited for: 3 -> 3; matrix products, arithmetic and copies ran while one was open for 0% -> 0% of each run, Pallas kernels for 2% -> 8%
where the time goes in v3:
time: 17.9 us; the launch traced here: 17.7 us
  starting transfers between devices  9.45 us (53%)
  Pallas kernels  4.06 us (23%)
  waiting for transfers between devices  3.52 us (20%)
  between operations  0.68 us (4%)
    ppermute x7, starting transfers between devices, xor_permute(): return lax.ppermute(value, GROUP, pairs)  9.45 us
    pallas_call x4, Pallas kernels, call(): pl.pallas_call(kernel, out_shape=outs, in_specs=[VMEM] * len(operands) +...  4.06 us
    ppermute x7, waiting for transfers between devices, xor_permute(): return lax.ppermute(value, GROUP, pairs)  3.52 us
  transfers between devices with their start and end apart: 7, of which 3 were waited for; matrix products, arithmetic and copies ran while one was open for 0% of the time, Pallas kernels for 8%

profile of v3, /device:TPU:0, one launch (start us, length us, event | category | flops | bytes accessed | tf_op | source)
XLA Modules:
  0.0 17.7 jit_solution(2350707610279228665)
XLA Ops:
  0.6 1.0 %shard_map.131 = (bf16[128,128]{1,0:T(8,128)(2,1)S(1)}, bf16[128,128]{1,0:T(8,128)(2,1)S(1)}, bf16[64,128]{1,0:T(8,128)(2,1)S(1)}) custom-call(bf16[128,128]{1,0:T(8,128)(2,1)} %refs_0_.1, s32[4,128]{1,0:T(4,128)} %bitcast.8, bf16[64,128]{1,0:T(8,128)(2,1)} %bitcast.6, s32[2,128]{1,0:T(2,128)} %bitcast.9, s32[16]{0:T(128)} %refs_4_.2), custom_call_target="tpu_custom_call" | custom-call | flops 65536 | bytes 199680 | tf_op jit(solution)/shard_map/pallas_call | solution.py:256
  1.6 3.6 %collective-permute-start.1 = (bf16[128,128]{1,0:T(8,128)(2,1)S(1)}, bf16[128,128]{1,0:T(8,128)(2,1)S(1)}, u32[]{:S(2)}, u32[]{:S(2)}) collective-permute-start(bf16[128,128]{1,0:T(8,128)(2,1)S(1)} %get-tuple-element.17.refs_0_), channel_id=1, source_target_pairs={{0,9},{1,8},{2,11},{3,10},{4,13},{5,12},{6,15},{7,14},{8,1},{9,0},... | collective-permute-start | bytes 98312 | tf_op jit(solution)/shard_map/ppermute | solution.py:33
  5.2 1.9 %collective-permute-start = (bf16[128,128]{1,0:T(8,128)(2,1)S(1)}, bf16[128,128]{1,0:T(8,128)(2,1)S(1)}, u32[]{:S(2)}, u32[]{:S(2)}) collective-permute-start(bf16[128,128]{1,0:T(8,128)(2,1)S(1)} %get-tuple-element.17.refs_0_), channel_id=1, source_target_pairs={{0,5},{1,4},{2,7},{3,6},{4,1},{5,0},{6,3},{7,2},{8,13},{9,12},{10,... | collective-permute-start | bytes 98312 | tf_op jit(solution)/shard_map/ppermute | solution.py:33
  7.0 0.0 collective-permute-done.1.refs_2_
  7.0 1.9 %collective-permute-start.2 = (bf16[128,128]{1,0:T(8,128)(2,1)S(1)}, bf16[128,128]{1,0:T(8,128)(2,1)S(1)}, u32[]{:S(2)}, u32[]{:S(2)}) collective-permute-start(bf16[128,128]{1,0:T(8,128)(2,1)S(1)} %collective-permute-done.1.refs_2_), channel_id=1, source_target_pairs={{0,5},{1,4},{2,7},{3,6},{4,1},{5,0},{6,3},{7,2},{8,13},{9,12},{10,... | collective-permute-start | bytes 98312 | tf_op jit(solution)/shard_map/ppermute | solution.py:33
  9.0 0.2 %collective-permute-start.3 = (bf16[64,128]{1,0:T(8,128)(2,1)S(1)}, bf16[64,128]{1,0:T(8,128)(2,1)S(1)}, u32[]{:S(2)}, u32[]{:S(2)}) collective-permute-start(bf16[64,128]{1,0:T(8,128)(2,1)S(1)} %get-tuple-element.19.refs_0_), channel_id=1, source_target_pairs={{0,1},{1,0},{2,3},{3,2},{4,5},{5,4},{6,7},{7,6},{8,9},{9,8},{10,11... | collective-permute-start | bytes 49160 | tf_op jit(solution)/shard_map/ppermute | solution.py:33
  9.2 1.0 %collective-permute-done.3.refs_1_ = bf16[64,128]{1,0:T(8,128)(2,1)S(1)} collective-permute-done((bf16[64,128]{1,0:T(8,128)(2,1)S(1)}, bf16[64,128]{1,0:T(8,128)(2,1)S(1)}, u32[]{:S(2)}, u32[]{:S(2)}) %collective-permute-start.3) | collective-permute-done | bytes 16416 | tf_op jit(solution)/shard_map/ppermute | solution.py:33
  10.2 1.4 %shard_map.132 = (bf16[128,128]{1,0:T(8,128)(2,1)S(1)}, bf16[1024,128]{1,0:T(8,128)(2,1)S(1)}, bf16[1024,128]{1,0:T(8,128)(2,1)S(1)}, f32[1,128]{1,0:T(1,128)S(1...) custom-call(bf16[64,128]{1,0:T(8,128)(2,1)S(1)} %get-tuple-element.1, ...), custom_call_target="tpu_custom_call" | custom-call | flops 65536 | bytes 1557248 | tf_op jit(solution)/shard_map/pallas_call | solution.py:256
  11.5 0.0 collective-permute-done.refs_1_
  11.5 0.0 collective-permute-done.2.refs_3_
  11.5 0.6 %shard_map.133 = (f32[16,128]{1,0:T(8,128)S(1)}, f32[16,128]{1,0:T(8,128)S(1)}, f32[32,128]{1,0:T(8,128)S(1)}) custom-call(bf16[128,128]{1,0:T(8,128)(2,1)S(1)} %get-tuple-element.17.refs_0_, bf16[128,128]{1,0:T(8,128)(2,1)S(1)} %collective-permute-done.refs_1_, bf16[128,128]{1,0:T(8,128)(2,1)S(1)} %collective-permute-done.1.refs_2_, ...), custom_call_target="tpu_custom_call" | custom-call | flops 134217728 | bytes 1015808 | tf_op jit(solution)/shard_map/pallas_call | solution.py:256
  12.1 1.4 %collective-permute-start.5 = (f32[32,128]{1,0:T(8,128)S(1)}, f32[32,128]{1,0:T(8,128)S(1)}, u32[]{:S(2)}, u32[]{:S(2)}) collective-permute-start(f32[32,128]{1,0:T(8,128)S(1)} %get-tuple-element.25), channel_id=1, source_target_pairs={{0,3},{1,2},{2,1},{3,0},{4,7},{5,6},{6,5},{7,4},{8,11},{9,10},{10,... | collective-permute-start | bytes 49160 | tf_op jit(solution)/shard_map/ppermute | solution.py:33
  13.5 0.3 %collective-permute-start.4 = (f32[16,128]{1,0:T(8,128)S(1)}, f32[16,128]{1,0:T(8,128)S(1)}, u32[]{:S(2)}, u32[]{:S(2)}) collective-permute-start(f32[16,128]{1,0:T(8,128)S(1)} %get-tuple-element.24), channel_id=1, source_target_pairs={{0,1},{1,0},{2,3},{3,2},{4,5},{5,4},{6,7},{7,6},{8,9},{9,8},{10,11... | collective-permute-start | bytes 24584 | tf_op jit(solution)/shard_map/ppermute | solution.py:33
  13.8 1.6 %collective-permute-done.5.chip_ref = f32[32,128]{1,0:T(8,128)S(1)} collective-permute-done((f32[32,128]{1,0:T(8,128)S(1)}, f32[32,128]{1,0:T(8,128)S(1)}, u32[]{:S(2)}, u32[]{:S(2)}) %collective-permute-start.5) | collective-permute-done | bytes 16416 | tf_op jit(solution)/shard_map/ppermute | solution.py:33
  15.3 0.2 %collective-permute-start.6 = (f32[16,128]{1,0:T(8,128)S(1)}, f32[16,128]{1,0:T(8,128)S(1)}, u32[]{:S(2)}, u32[]{:S(2)}) collective-permute-start(f32[16,128]{1,0:T(8,128)S(1)} %slice.4), channel_id=1, source_target_pairs={{0,1},{1,0},{2,3},{3,2},{4,5},{5,4},{6,7},{7,6},{8,9},{9,8},{10,11... | collective-permute-start | bytes 24584 | tf_op jit(solution)/shard_map/ppermute | solution.py:33
  15.5 0.0 collective-permute-done.4.core_ref
  15.5 1.0 %collective-permute-done.6.relay_ref = f32[16,128]{1,0:T(8,128)S(1)} collective-permute-done((f32[16,128]{1,0:T(8,128)S(1)}, f32[16,128]{1,0:T(8,128)S(1)}, u32[]{:S(2)}, u32[]{:S(2)}) %collective-permute-start.6) | collective-permute-done | bytes 8224 | tf_op jit(solution)/shard_map/ppermute | solution.py:33
  16.5 1.2 %shard_map.134 = (bf16[1,2048]{1,0:T(2,128)(2,1)}, f32[1,1024]{1,0:T(1,128)}) custom-call(f32[16,128]{1,0:T(8,128)S(1)} %get-tuple-element.23.keep_ref, f32[16,128]{1,0:T(8,128)S(1)} %collective-permute-done.4.core_ref, f32[32,128]{1,0:T(8,128)S(1)} %collective-permute-done.5.chip_ref, f32[16,128]{1,0:T(8,128)S(1)} %collective-permute-done.6.relay_ref, ...), custom_call_target="tpu_custom_call" | custom-call | flops 33554432 | bytes 459520 | tf_op jit(solution)/shard_map/pallas_call | solution.py:256
  (1 shorter events, 0.0 us)
Async XLA Ops:
  1.6 5.4 %collective-permute-start.1 = (bf16[128,128]{1,0:T(8,128)(2,1)S(1)}, bf16[128,128]{1,0:T(8,128)(2,1)S(1)}, u32[]{:S(2)}, u32[]{:S(2)}) collective-permute-start(bf16[128,128]{1,0:T(8,128)(2,1)S(1)} %get-tuple-element.17.refs_0_), channel_id=1, source_target_pairs={{0,9},{1,8},{2,11},{3,10},{4,13},{5,12},{6,15},{7,14},{8,1},{9,0},... | collective-permute-start | bytes 98312 | tf_op jit(solution)/shard_map/ppermute | solution.py:33
  5.2 6.4 %collective-permute-start = (bf16[128,128]{1,0:T(8,128)(2,1)S(1)}, bf16[128,128]{1,0:T(8,128)(2,1)S(1)}, u32[]{:S(2)}, u32[]{:S(2)}) collective-permute-start(bf16[128,128]{1,0:T(8,128)(2,1)S(1)} %get-tuple-element.17.refs_0_), channel_id=1, source_target_pairs={{0,5},{1,4},{2,7},{3,6},{4,1},{5,0},{6,3},{7,2},{8,13},{9,12},{10,... | collective-permute-start | bytes 98312 | tf_op jit(solution)/shard_map/ppermute | solution.py:33
  7.0 4.5 %collective-permute-start.2 = (bf16[128,128]{1,0:T(8,128)(2,1)S(1)}, bf16[128,128]{1,0:T(8,128)(2,1)S(1)}, u32[]{:S(2)}, u32[]{:S(2)}) collective-permute-start(bf16[128,128]{1,0:T(8,128)(2,1)S(1)} %collective-permute-done.1.refs_2_), channel_id=1, source_target_pairs={{0,5},{1,4},{2,7},{3,6},{4,1},{5,0},{6,3},{7,2},{8,13},{9,12},{10,... | collective-permute-start | bytes 98312 | tf_op jit(solution)/shard_map/ppermute | solution.py:33
  9.0 1.2 %collective-permute-start.3 = (bf16[64,128]{1,0:T(8,128)(2,1)S(1)}, bf16[64,128]{1,0:T(8,128)(2,1)S(1)}, u32[]{:S(2)}, u32[]{:S(2)}) collective-permute-start(bf16[64,128]{1,0:T(8,128)(2,1)S(1)} %get-tuple-element.19.refs_0_), channel_id=1, source_target_pairs={{0,1},{1,0},{2,3},{3,2},{4,5},{5,4},{6,7},{7,6},{8,9},{9,8},{10,11... | collective-permute-start | bytes 49160 | tf_op jit(solution)/shard_map/ppermute | solution.py:33
  12.1 3.2 %collective-permute-start.5 = (f32[32,128]{1,0:T(8,128)S(1)}, f32[32,128]{1,0:T(8,128)S(1)}, u32[]{:S(2)}, u32[]{:S(2)}) collective-permute-start(f32[32,128]{1,0:T(8,128)S(1)} %get-tuple-element.25), channel_id=1, source_target_pairs={{0,3},{1,2},{2,1},{3,0},{4,7},{5,6},{6,5},{7,4},{8,11},{9,10},{10,... | collective-permute-start | bytes 49160 | tf_op jit(solution)/shard_map/ppermute | solution.py:33
  13.5 2.1 %collective-permute-start.4 = (f32[16,128]{1,0:T(8,128)S(1)}, f32[16,128]{1,0:T(8,128)S(1)}, u32[]{:S(2)}, u32[]{:S(2)}) collective-permute-start(f32[16,128]{1,0:T(8,128)S(1)} %get-tuple-element.24), channel_id=1, source_target_pairs={{0,1},{1,0},{2,3},{3,2},{4,5},{5,4},{6,7},{7,6},{8,9},{9,8},{10,11... | collective-permute-start | bytes 24584 | tf_op jit(solution)/shard_map/ppermute | solution.py:33
  15.3 1.2 %collective-permute-start.6 = (f32[16,128]{1,0:T(8,128)S(1)}, f32[16,128]{1,0:T(8,128)S(1)}, u32[]{:S(2)}, u32[]{:S(2)}) collective-permute-start(f32[16,128]{1,0:T(8,128)S(1)} %slice.4), channel_id=1, source_target_pairs={{0,1},{1,0},{2,3},{3,2},{4,5},{5,4},{6,7},{7,6},{8,9},{9,8},{10,11... | collective-permute-start | bytes 24584 | tf_op jit(solution)/shard_map/ppermute | solution.py:33

commit v4 on v3

--- a/solution.py
+++ b/solution.py
@@ -62,63 +62,30 @@
     fold = channels // ROWS
     tile, sub = lax.axis_index("tile"), lax.axis_index("sub")
     mine = row_in_tile(sub_count)
+    half = fold * piece * ROWS
     right = right_ref[...].astype(jnp.float32)
     right_scale = jnp.exp2(right_exp_ref[...].astype(jnp.float32))
     first = tile * band + sub * piece
-    scaled = []
     for j in range(piece):
         scale = right_scale[j : j + 1] * mask_ref[first + j].astype(jnp.float32)
-        scaled.append(right[j * channels : (j + 1) * channels] * scale)
-        right_out[j * channels : (j + 1) * channels, :] = scaled[j].astype(jnp.bfloat16)
-    half = fold * piece * ROWS
-    for x in range(fold):
-        rows = jnp.concatenate([scaled[j][x * ROWS : (x + 1) * ROWS] for j in range(piece)], axis=0)
-        at = half + x * piece * ROWS
-        block_ref[at : at + piece * ROWS, :] = rows.astype(jnp.bfloat16)
+        scaled = (right[j * channels : (j + 1) * channels] * scale).astype(jnp.bfloat16)
+        right_out[j * channels : (j + 1) * channels, :] = scaled
+        block_ref[half + j * channels : half + (j + 1) * channels, :] = scaled
     left = jnp.transpose(left_ref[...].astype(jnp.float32))
     left_scale = jnp.exp2(left_exp_ref[...].astype(jnp.float32))
     for i in range(band):
         scale = left_scale[i : i + 1] * mask_ref[tile * band + i].astype(jnp.float32)
         left_f32[i * channels : (i + 1) * channels, :] = left[i * channels : (i + 1) * channels] * scale
-    for x in range(fold):
-        rows = []
-        for j in range(piece):
-            at = pl.multiple_of((sub * piece + j) * channels + x * ROWS, ROWS)
-            rows.append(left_f32[pl.ds(at, ROWS), :])
-        at = x * piece * ROWS
-        block_ref[at : at + piece * ROWS, :] = jnp.concatenate(rows, axis=0).astype(jnp.bfloat16)
-    for i in range(band):
-        at = pl.multiple_of((mine ^ i) * channels, channels)
-        left_out[i * channels : (i + 1) * channels, :] = left_f32[pl.ds(at, channels), :].astype(jnp.bfloat16)
-
-
-def arrange_kernel(dims, *refs):
-    channels, _, sub_count = dims
-    params = (len(refs) - 7) // 2
-    right_ref, other_ref = refs[:2]
-    sources, refs = refs[2 : 2 + params], refs[2 + params :]
-    right_out, swapped_out = refs[:2]
-    targets, (both, weight_f32, semaphores) = refs[2 : 2 + params], refs[2 + params :]
-    copies = fetch(sources, targets, semaphores)
-    seqs = right_ref.shape[1]
-    piece = right_ref.shape[0] // channels
-    fold = channels // ROWS
-    sub = lax.axis_index("sub")
-    mine = row_in_tile(sub_count)
-    both[sub] = right_ref[...].reshape(piece, channels, seqs)
-    both[1 - sub] = other_ref[...].reshape(piece, channels, seqs)
-    for i in range(right_out.shape[0] // channels):
-        here = mine ^ i
-        right_out[i * channels : (i + 1) * channels, :] = both[here // piece, here % piece]
-    copies[0].wait()
-    weight_f32[...] = targets[0][...].astype(jnp.float32)
-    for g in range(ROWS):
+    for target, places in (
+        (block_ref, [sub * piece + j for j in range(piece)]),
+        (left_out, [mine ^ i for i in range(band)]),
+    ):
         for x in range(fold):
-            at = (g * fold + x) * channels
-            rows = weight_f32[pl.ds(x * ROWS + g, channels, stride=channels), :]
-            swapped_out[at : at + channels, :] = rows.astype(jnp.bfloat16)
-    for copy in copies[1:]:
-        copy.wait()
+            rows = [
+                left_f32[pl.ds(pl.multiple_of(place * channels + x * ROWS, ROWS), ROWS), :] for place in places
+            ]
+            at = x * len(places) * ROWS
+            target[at : at + len(places) * ROWS, :] = jnp.concatenate(rows, axis=0).astype(jnp.bfloat16)
 
 
 def trade_chunks(arrays, width):
@@ -134,28 +101,34 @@
     return arrays
 
 
-def pair_kernel(dims, block_count, *refs):
-    channels, _, sub_count = dims
-    blocks = refs[:block_count]
-    left_ref, right_ref, weight_ref, swapped_ref, keep_ref, core_ref, chip_ref, outer = refs[block_count:]
+def pair_terms(channels, blocks, left_ref, right_ref, weight_ref, scratch, store, ready):
     fold = channels // ROWS
-    half = blocks[0].shape[0] // 2
-    size = half // fold
-    count = block_count * size // ROWS
-    rows = count * ROWS
-    band = left_ref.shape[0] // channels
-    for way, own in enumerate((left_ref, right_ref)):
-        base = half * (1 - way)
-        factor = jnp.concatenate(
-            [b[base + x * size : base + (x + 1) * size, :] for x in range(fold) for b in blocks], axis=0
-        )
-        product = lax.dot_general(factor, own[...], NT, preferred_element_type=jnp.float32)
-        for i in range(0, band, fold):
-            lanes = slice(i * channels, i * channels + LANES)
-            parts = [product[x * rows : (x + 1) * rows, lanes] for x in range(fold)]
-            for n, part in enumerate(trade_chunks(parts, channels)):
-                outer[way * band + i + n] = part
-    natural = jnp.concatenate(
+    piece = (blocks[0].shape[0] // channels) // 2
+    half = piece * channels
+    band = right_ref.shape[0] // channels
+    count = len(blocks) * piece
+    padded = blocks + [blocks[-1]] * (-len(blocks) % (fold // math.gcd(fold, piece)))
+    left_blocks = jnp.concatenate(
+        [b[x * piece * ROWS : (x + 1) * piece * ROWS, :] for x in range(fold) for b in blocks], axis=0
+    )
+    right_blocks = jnp.concatenate([b[half:, :] for b in padded], axis=0)
+    size = count * band * ROWS
+    for way, (rows, columns) in enumerate(((left_ref[...], right_blocks), (left_blocks, right_ref[...]))):
+        product = lax.dot_general(rows, columns, NT, preferred_element_type=jnp.float32)
+        inner = product.shape[0] // fold
+        for n in range(0, product.shape[1], LANES):
+            parts = [product[x * inner : (x + 1) * inner, n : n + LANES] for x in range(fold)]
+            for m, part in enumerate(trade_chunks(parts, channels)):
+                at = (n // channels + m) * inner
+                if at < size:
+                    scratch[way * size + at : way * size + at + inner, :] = part
+    flat = jnp.concatenate(
+        [scratch[pl.ds(g, 2 * band * count, stride=ROWS), :] for g in range(ROWS)], axis=1
+    )
+    high = flat.astype(jnp.bfloat16)
+    low = (flat - high.astype(jnp.float32)).astype(jnp.bfloat16)
+    ready()
+    weight = jnp.concatenate(
         [
             weight_ref[(x * ROWS + g) * channels : (x * ROWS + g + 1) * channels, :]
             for g in range(ROWS)
@@ -163,26 +136,55 @@
         ],
         axis=0,
     )
-    for way, weight in enumerate((swapped_ref[...], natural)):
-        flat = jnp.concatenate(
-            [
-                jnp.concatenate(
-                    [outer[way * band + i, pl.ds(g, count, stride=ROWS), :] for g in range(ROWS)],
-                    axis=1,
-                )
-                for i in range(band)
-            ],
-            axis=0,
-        )
-        high = flat.astype(jnp.bfloat16)
-        low = (flat - high.astype(jnp.float32)).astype(jnp.bfloat16)
-        terms = jnp.dot(jnp.concatenate([high, low], axis=0), weight, preferred_element_type=jnp.float32)
-        terms = terms[: band * count] + terms[band * count :]
-        place = lambda i: slice(i * count, (i + 1) * count)
-        keep_ref[place(way), :] = terms[place(0)]
-        core_ref[place(way), :] = terms[place(1)]
-        for i in range(sub_count, band):
-            chip_ref[place((i - sub_count) * 2 + way), :] = terms[place(i)]
+    terms = jnp.dot(jnp.concatenate([high, low], axis=0), weight, preferred_element_type=jnp.float32)
+    terms = terms[: 2 * band * count] + terms[2 * band * count :]
+    scratch[: band * count, :] = terms[: band * count]
+    for i in range(band):
+        store(i, 0, scratch[pl.ds(i, count, stride=band), :])
+        store(i, 1, terms[(band + i) * count : (band + i + 1) * count])
+
+
+def early_kernel(dims, block_count, total, *refs):
+    channels, _, sub_count = dims
+    blocks, (left_ref, right_ref, other_ref), refs = refs[:block_count], refs[block_count:][:3], refs[block_count + 3 :]
+    params = (len(refs) - 5) // 2
+    sources, (terms_out, right_out), refs = refs[:params], refs[params:][:2], refs[params + 2 :]
+    targets, (both, scratch, semaphores) = refs[:params], refs[params:]
+    copies = fetch(sources, targets, semaphores)
+    seqs = right_ref.shape[1]
+    piece = right_ref.shape[0] // channels
+    sub = lax.axis_index("sub")
+    mine = row_in_tile(sub_count)
+    both[sub] = right_ref[...].reshape(piece, channels, seqs)
+    both[1 - sub] = other_ref[...].reshape(piece, channels, seqs)
+    for i in range(right_out.shape[0] // channels):
+        here = mine ^ i
+        right_out[i * channels : (i + 1) * channels, :] = both[here // piece, here % piece]
+
+    def store(i, way, terms):
+        at = (i * 2 + way) * total
+        terms_out[at : at + terms.shape[0], :] = terms
+
+    pair_terms(channels, list(blocks), left_ref, right_out, targets[0], scratch, store, copies[0].wait)
+    for copy in copies[1:]:
+        copy.wait()
+
+
+def late_kernel(dims, block_count, total, *refs):
+    channels, depth_count, _ = dims
+    blocks, (left_ref, right_ref, weight_ref, terms_ref) = refs[:block_count], refs[block_count : block_count + 4]
+    keep_ref, core_ref, chip_ref, scratch = refs[block_count + 4 :]
+    keep_ref[...] = terms_ref[: 2 * total, :]
+    core_ref[...] = terms_ref[2 * total : 4 * total, :]
+    if depth_count > 1:
+        chip_ref[...] = terms_ref[4 * total :, :]
+
+    def store(i, way, terms):
+        target = (keep_ref, core_ref, chip_ref)[min(i, 2)]
+        at = (max(i - 2, 0) * 2 + way + 1) * total
+        target[at - terms.shape[0] : at, :] = terms
+
+    pair_terms(channels, list(blocks), left_ref, right_ref, weight_ref, scratch, store, lambda: None)
 
 
 def finish_kernel(
@@ -319,6 +321,9 @@
         for bits in list(blocks):
             blocks[bits ^ bit] = xor_permute(blocks[bits], bit, 0, 1)
     other_rows = xor_permute(right_rows, 0, 0, 1)
+    order = list(blocks)
+    early, late = order[: max(len(order) * 3 // 4, 1)], order[max(len(order) * 3 // 4, 1) :]
+    count = len(order) * piece
     params = (
         out_weight,
         out_bias.reshape(1, -1),
@@ -328,35 +333,34 @@
         distogram_weight.T,
         distogram_bias.reshape(1, -1),
     )
-    right_rows, swapped, weight, *params = call(
-        functools.partial(arrange_kernel, dims),
-        1 << 16,
+    terms, right_rows, weight, *params = call(
+        functools.partial(early_kernel, dims, len(early), count),
+        1 << 26,
         (
+            shape(band * 2 * count, pair_channels, f32),
             shape(band * channels, seqs, bf16),
-            shape(*out_weight.shape, bf16),
             *(shape(*p.shape, p.dtype) for p in params),
         ),
         [
             pltpu.VMEM((sub_count, piece, channels, seqs), bf16),
-            pltpu.VMEM(out_weight.shape, f32),
+            pltpu.VMEM((2 * band * len(early) * piece * ROWS, LANES), f32),
             pltpu.SemaphoreType.DMA((len(params),)),
         ],
-        (right_rows, other_rows),
+        (*(blocks[k] for k in early), left_rows, right_rows, other_rows),
         params,
     )
-    block_tiles = tuple(sorted(blocks))
-    count = len(block_tiles) * piece
     keep, core, chip = call(
-        functools.partial(pair_kernel, dims, len(block_tiles)),
-        1 << 27,
+        functools.partial(late_kernel, dims, len(late), count),
+        1 << 26,
         (
             shape(2 * count, pair_channels, f32),
             shape(2 * count, pair_channels, f32),
             shape(max(band - sub_count, 1) * 2 * count, pair_channels, f32),
         ),
-        [pltpu.VMEM((2 * band, count * ROWS, LANES), f32)],
-        (*(blocks[k] for k in block_tiles), left_rows, right_rows, weight, swapped),
-    )
+        [pltpu.VMEM((2 * band * len(late) * piece * ROWS, LANES), f32)],
+        (*(blocks[k] for k in late), left_rows, right_rows, weight, terms),
+    )
+    block_tiles = tuple(order)
     size = sub_count * 2 * count
     for bit in bits_of(depth_count)[:-1]:
         rows = jnp.concatenate([keep, core, chip], axis=0)

time: 17.9 us -> 17.8 us (level)
  transfers between devices with their start and end apart: 7 -> 7, of which waited for: 3 -> 3; matrix products, arithmetic and copies ran while one was open for 0% -> 0% of each run, Pallas kernels for 8% -> 7%
where the time goes in v4:
time: 17.8 us; the launch traced here: 17.5 us
  starting transfers between devices  9.46 us (53%)
  Pallas kernels  3.91 us (22%)
  waiting for transfers between devices  3.5 us (20%)
  between operations  0.67 us (4%)
    ppermute x7, starting transfers between devices, xor_permute(): return lax.ppermute(value, GROUP, pairs)  9.46 us
    pallas_call x4, Pallas kernels, call(): pl.pallas_call(kernel, out_shape=outs, in_specs=[VMEM] * len(operands) +...  3.91 us
    ppermute x7, waiting for transfers between devices, xor_permute(): return lax.ppermute(value, GROUP, pairs)  3.5 us
  transfers between devices with their start and end apart: 7, of which 3 were waited for; matrix products, arithmetic and copies ran while one was open for 0% of the time, Pallas kernels for 7%

profile of v4, /device:TPU:0, one launch (start us, length us, event | category | flops | bytes accessed | tf_op | source)
XLA Modules:
  0.0 17.5 jit_solution(2616549665546982397)
XLA Ops:
  0.6 1.0 %shard_map.131 = (bf16[128,128]{1,0:T(8,128)(2,1)S(1)}, bf16[128,128]{1,0:T(8,128)(2,1)S(1)}, bf16[64,128]{1,0:T(8,128)(2,1)S(1)}) custom-call(bf16[128,128]{1,0:T(8,128)(2,1)} %refs_0_.1, s32[4,128]{1,0:T(4,128)} %bitcast.8, bf16[64,128]{1,0:T(8,128)(2,1)} %bitcast.6, s32[2,128]{1,0:T(2,128)} %bitcast.9, s32[16]{0:T(128)} %refs_4_.1), custom_call_target="tpu_custom_call" | custom-call | flops 65536 | bytes 199680 | tf_op jit(solution)/shard_map/pallas_call | solution.py:258
  1.6 3.6 %collective-permute-start = (bf16[128,128]{1,0:T(8,128)(2,1)S(1)}, bf16[128,128]{1,0:T(8,128)(2,1)S(1)}, u32[]{:S(2)}, u32[]{:S(2)}) collective-permute-start(bf16[128,128]{1,0:T(8,128)(2,1)S(1)} %get-tuple-element.17.refs_0_), channel_id=1, source_target_pairs={{0,9},{1,8},{2,11},{3,10},{4,13},{5,12},{6,15},{7,14},{8,1},{9,0},... | collective-permute-start | bytes 98312 | tf_op jit(solution)/shard_map/ppermute | solution.py:33
  5.2 1.9 %collective-permute-start.2 = (bf16[128,128]{1,0:T(8,128)(2,1)S(1)}, bf16[128,128]{1,0:T(8,128)(2,1)S(1)}, u32[]{:S(2)}, u32[]{:S(2)}) collective-permute-start(bf16[128,128]{1,0:T(8,128)(2,1)S(1)} %get-tuple-element.17.refs_0_), channel_id=1, source_target_pairs={{0,5},{1,4},{2,7},{3,6},{4,1},{5,0},{6,3},{7,2},{8,13},{9,12},{10,... | collective-permute-start | bytes 98312 | tf_op jit(solution)/shard_map/ppermute | solution.py:33
  7.0 0.0 collective-permute-done.refs_1_
  7.0 1.9 %collective-permute-start.1 = (bf16[128,128]{1,0:T(8,128)(2,1)S(1)}, bf16[128,128]{1,0:T(8,128)(2,1)S(1)}, u32[]{:S(2)}, u32[]{:S(2)}) collective-permute-start(bf16[128,128]{1,0:T(8,128)(2,1)S(1)} %collective-permute-done.refs_1_), channel_id=1, source_target_pairs={{0,5},{1,4},{2,7},{3,6},{4,1},{5,0},{6,3},{7,2},{8,13},{9,12},{10,... | collective-permute-start | bytes 98312 | tf_op jit(solution)/shard_map/ppermute | solution.py:33
  9.0 0.2 %collective-permute-start.3 = (bf16[64,128]{1,0:T(8,128)(2,1)S(1)}, bf16[64,128]{1,0:T(8,128)(2,1)S(1)}, u32[]{:S(2)}, u32[]{:S(2)}) collective-permute-start(bf16[64,128]{1,0:T(8,128)(2,1)S(1)} %get-tuple-element.19.refs_4_), channel_id=1, source_target_pairs={{0,1},{1,0},{2,3},{3,2},{4,5},{5,4},{6,7},{7,6},{8,9},{9,8},{10,11... | collective-permute-start | bytes 49160 | tf_op jit(solution)/shard_map/ppermute | solution.py:33
  9.2 1.0 %collective-permute-done.3.refs_5_ = bf16[64,128]{1,0:T(8,128)(2,1)S(1)} collective-permute-done((bf16[64,128]{1,0:T(8,128)(2,1)S(1)}, bf16[64,128]{1,0:T(8,128)(2,1)S(1)}, u32[]{:S(2)}, u32[]{:S(2)}) %collective-permute-start.3) | collective-permute-done | bytes 16416 | tf_op jit(solution)/shard_map/ppermute | solution.py:33
  10.2 0.0 collective-permute-done.2.refs_2_
  10.2 1.3 %shard_map.132 = (f32[64,128]{1,0:T(8,128)S(1)}, bf16[128,128]{1,0:T(8,128)(2,1)S(1)}, bf16[1024,128]{1,0:T(8,128)(2,1)S(1)}, f32[1,128]{1,0:T(1,128)S(1)}, bf16...) custom-call(bf16[128,128]{1,0:T(8,128)(2,1)S(1)} %get-tuple-element., ...), custom_call_target="tpu_custom_call" | custom-call | flops 67108864 | bytes 1131264 | tf_op jit(solution)/shard_map/pallas_call | solution.py:258
  11.5 0.0 collective-permute-done.1.refs_0_
  11.5 0.5 %shard_map.133 = (f32[16,128]{1,0:T(8,128)S(1)}, f32[16,128]{1,0:T(8,128)S(1)}, f32[32,128]{1,0:T(8,128)S(1)}) custom-call(bf16[128,128]{1,0:T(8,128)(2,1)S(1)} %collective-permute-done.1.refs_0_, bf16[128,128]{1,0:T(8,128)(2,1)S(1)} %get-tuple-element.18.refs_3_.refs_1_, bf16[128,128]{1,0:T(8,128)(2,1)S(1)} %get-tuple-element.20.refs_2_, ...), custom_call_target="tpu_custom_call" | custom-call | flops 67108864 | bytes 491520 | tf_op jit(solution)/shard_map/pallas_call | solution.py:258
  12.0 1.4 %collective-permute-start.5 = (f32[32,128]{1,0:T(8,128)S(1)}, f32[32,128]{1,0:T(8,128)S(1)}, u32[]{:S(2)}, u32[]{:S(2)}) collective-permute-start(f32[32,128]{1,0:T(8,128)S(1)} %get-tuple-element.25), channel_id=1, source_target_pairs={{0,3},{1,2},{2,1},{3,0},{4,7},{5,6},{6,5},{7,4},{8,11},{9,10},{10,... | collective-permute-start | bytes 49160 | tf_op jit(solution)/shard_map/ppermute | solution.py:33
  13.3 0.3 %collective-permute-start.4 = (f32[16,128]{1,0:T(8,128)S(1)}, f32[16,128]{1,0:T(8,128)S(1)}, u32[]{:S(2)}, u32[]{:S(2)}) collective-permute-start(f32[16,128]{1,0:T(8,128)S(1)} %get-tuple-element.24), channel_id=1, source_target_pairs={{0,1},{1,0},{2,3},{3,2},{4,5},{5,4},{6,7},{7,6},{8,9},{9,8},{10,11... | collective-permute-start | bytes 24584 | tf_op jit(solution)/shard_map/ppermute | solution.py:33
  13.6 1.6 %collective-permute-done.5.chip_ref = f32[32,128]{1,0:T(8,128)S(1)} collective-permute-done((f32[32,128]{1,0:T(8,128)S(1)}, f32[32,128]{1,0:T(8,128)S(1)}, u32[]{:S(2)}, u32[]{:S(2)}) %collective-permute-start.5) | collective-permute-done | bytes 16416 | tf_op jit(solution)/shard_map/ppermute | solution.py:33
  15.2 0.2 %collective-permute-start.6 = (f32[16,128]{1,0:T(8,128)S(1)}, f32[16,128]{1,0:T(8,128)S(1)}, u32[]{:S(2)}, u32[]{:S(2)}) collective-permute-start(f32[16,128]{1,0:T(8,128)S(1)} %slice.4), channel_id=1, source_target_pairs={{0,1},{1,0},{2,3},{3,2},{4,5},{5,4},{6,7},{7,6},{8,9},{9,8},{10,11... | collective-permute-start | bytes 24584 | tf_op jit(solution)/shard_map/ppermute | solution.py:33
  15.4 0.0 collective-permute-done.4.core_ref
  15.4 1.0 %collective-permute-done.6.relay_ref = f32[16,128]{1,0:T(8,128)S(1)} collective-permute-done((f32[16,128]{1,0:T(8,128)S(1)}, f32[16,128]{1,0:T(8,128)S(1)}, u32[]{:S(2)}, u32[]{:S(2)}) %collective-permute-start.6) | collective-permute-done | bytes 8224 | tf_op jit(solution)/shard_map/ppermute | solution.py:33
  16.4 1.2 %shard_map.134 = (bf16[1,2048]{1,0:T(2,128)(2,1)}, f32[1,1024]{1,0:T(1,128)}) custom-call(f32[16,128]{1,0:T(8,128)S(1)} %get-tuple-element.23.keep_ref, f32[16,128]{1,0:T(8,128)S(1)} %collective-permute-done.4.core_ref, f32[32,128]{1,0:T(8,128)S(1)} %collective-permute-done.5.chip_ref, f32[16,128]{1,0:T(8,128)S(1)} %collective-permute-done.6.relay_ref, ...), custom_call_target="tpu_custom_call" | custom-call | flops 33554432 | bytes 459520 | tf_op jit(solution)/shard_map/pallas_call | solution.py:258
  (1 shorter events, 0.0 us)
Async XLA Ops:
  1.6 5.4 %collective-permute-start = (bf16[128,128]{1,0:T(8,128)(2,1)S(1)}, bf16[128,128]{1,0:T(8,128)(2,1)S(1)}, u32[]{:S(2)}, u32[]{:S(2)}) collective-permute-start(bf16[128,128]{1,0:T(8,128)(2,1)S(1)} %get-tuple-element.17.refs_0_), channel_id=1, source_target_pairs={{0,9},{1,8},{2,11},{3,10},{4,13},{5,12},{6,15},{7,14},{8,1},{9,0},... | collective-permute-start | bytes 98312 | tf_op jit(solution)/shard_map/ppermute | solution.py:33
  5.2 5.0 %collective-permute-start.2 = (bf16[128,128]{1,0:T(8,128)(2,1)S(1)}, bf16[128,128]{1,0:T(8,128)(2,1)S(1)}, u32[]{:S(2)}, u32[]{:S(2)}) collective-permute-start(bf16[128,128]{1,0:T(8,128)(2,1)S(1)} %get-tuple-element.17.refs_0_), channel_id=1, source_target_pairs={{0,5},{1,4},{2,7},{3,6},{4,1},{5,0},{6,3},{7,2},{8,13},{9,12},{10,... | collective-permute-start | bytes 98312 | tf_op jit(solution)/shard_map/ppermute | solution.py:33
  7.0 4.4 %collective-permute-start.1 = (bf16[128,128]{1,0:T(8,128)(2,1)S(1)}, bf16[128,128]{1,0:T(8,128)(2,1)S(1)}, u32[]{:S(2)}, u32[]{:S(2)}) collective-permute-start(bf16[128,128]{1,0:T(8,128)(2,1)S(1)} %collective-permute-done.refs_1_), channel_id=1, source_target_pairs={{0,5},{1,4},{2,7},{3,6},{4,1},{5,0},{6,3},{7,2},{8,13},{9,12},{10,... | collective-permute-start | bytes 98312 | tf_op jit(solution)/shard_map/ppermute | solution.py:33
  9.0 1.2 %collective-permute-start.3 = (bf16[64,128]{1,0:T(8,128)(2,1)S(1)}, bf16[64,128]{1,0:T(8,128)(2,1)S(1)}, u32[]{:S(2)}, u32[]{:S(2)}) collective-permute-start(bf16[64,128]{1,0:T(8,128)(2,1)S(1)} %get-tuple-element.19.refs_4_), channel_id=1, source_target_pairs={{0,1},{1,0},{2,3},{3,2},{4,5},{5,4},{6,7},{7,6},{8,9},{9,8},{10,11... | collective-permute-start | bytes 49160 | tf_op jit(solution)/shard_map/ppermute | solution.py:33
  12.0 3.2 %collective-permute-start.5 = (f32[32,128]{1,0:T(8,128)S(1)}, f32[32,128]{1,0:T(8,128)S(1)}, u32[]{:S(2)}, u32[]{:S(2)}) collective-permute-start(f32[32,128]{1,0:T(8,128)S(1)} %get-tuple-element.25), channel_id=1, source_target_pairs={{0,3},{1,2},{2,1},{3,0},{4,7},{5,6},{6,5},{7,4},{8,11},{9,10},{10,... | collective-permute-start | bytes 49160 | tf_op jit(solution)/shard_map/ppermute | solution.py:33
  13.3 2.1 %collective-permute-start.4 = (f32[16,128]{1,0:T(8,128)S(1)}, f32[16,128]{1,0:T(8,128)S(1)}, u32[]{:S(2)}, u32[]{:S(2)}) collective-permute-start(f32[16,128]{1,0:T(8,128)S(1)} %get-tuple-element.24), channel_id=1, source_target_pairs={{0,1},{1,0},{2,3},{3,2},{4,5},{5,4},{6,7},{7,6},{8,9},{9,8},{10,11... | collective-permute-start | bytes 24584 | tf_op jit(solution)/shard_map/ppermute | solution.py:33
  15.2 1.2 %collective-permute-start.6 = (f32[16,128]{1,0:T(8,128)S(1)}, f32[16,128]{1,0:T(8,128)S(1)}, u32[]{:S(2)}, u32[]{:S(2)}) collective-permute-start(f32[16,128]{1,0:T(8,128)S(1)} %slice.4), channel_id=1, source_target_pairs={{0,1},{1,0},{2,3},{3,2},{4,5},{5,4},{6,7},{7,6},{8,9},{9,8},{10,11... | collective-permute-start | bytes 24584 | tf_op jit(solution)/shard_map/ppermute | solution.py:33

commit v5 on v4

--- a/solution.py
+++ b/solution.py
@@ -88,40 +88,31 @@
             target[at : at + len(places) * ROWS, :] = jnp.concatenate(rows, axis=0).astype(jnp.bfloat16)
 
 
-def trade_chunks(arrays, width):
-    chunk = lax.broadcasted_iota(jnp.int32, arrays[0].shape, 1) // width
-    for bit in bits_of(len(arrays)):
-        keep = (chunk & bit) == 0
-        for x in range(len(arrays)):
-            if x & bit:
-                continue
-            low, high = arrays[x], arrays[x | bit]
-            arrays[x] = jnp.where(keep, low, pltpu.roll(high, bit * width, 1))
-            arrays[x | bit] = jnp.where(keep, pltpu.roll(low, LANES - bit * width, 1), high)
-    return arrays
-
-
 def pair_terms(channels, blocks, left_ref, right_ref, weight_ref, scratch, store, ready):
     fold = channels // ROWS
     piece = (blocks[0].shape[0] // channels) // 2
     half = piece * channels
     band = right_ref.shape[0] // channels
     count = len(blocks) * piece
-    padded = blocks + [blocks[-1]] * (-len(blocks) % (fold // math.gcd(fold, piece)))
     left_blocks = jnp.concatenate(
         [b[x * piece * ROWS : (x + 1) * piece * ROWS, :] for x in range(fold) for b in blocks], axis=0
     )
-    right_blocks = jnp.concatenate([b[half:, :] for b in padded], axis=0)
+    right_blocks = jnp.concatenate([b[half:, :] for b in blocks], axis=0)
+    chunk = lax.broadcasted_iota(jnp.int32, (1, LANES), 1) // channels
     size = count * band * ROWS
     for way, (rows, columns) in enumerate(((left_ref[...], right_blocks), (left_blocks, right_ref[...]))):
-        product = lax.dot_general(rows, columns, NT, preferred_element_type=jnp.float32)
+        members = range(columns.shape[0] // channels)
+        wide = jnp.concatenate(
+            [columns[m * channels : (m + 1) * channels] for m in members for _ in range(fold)], axis=0
+        )
+        product = lax.dot_general(rows, wide, NT, preferred_element_type=jnp.float32)
         inner = product.shape[0] // fold
-        for n in range(0, product.shape[1], LANES):
-            parts = [product[x * inner : (x + 1) * inner, n : n + LANES] for x in range(fold)]
-            for m, part in enumerate(trade_chunks(parts, channels)):
-                at = (n // channels + m) * inner
-                if at < size:
-                    scratch[way * size + at : way * size + at + inner, :] = part
+        for m in members:
+            lanes = slice(m * LANES, (m + 1) * LANES)
+            value = product[:inner, lanes]
+            for x in range(1, fold):
+                value = jnp.where(chunk == x, product[x * inner : (x + 1) * inner, lanes], value)
+            scratch[way * size + m * inner : way * size + (m + 1) * inner, :] = value
     flat = jnp.concatenate(
         [scratch[pl.ds(g, 2 * band * count, stride=ROWS), :] for g in range(ROWS)], axis=1
     )
@@ -187,36 +178,8 @@
     pair_terms(channels, list(blocks), left_ref, right_ref, weight_ref, scratch, store, lambda: None)
 
 
-def finish_kernel(
-    dims,
-    block_tiles,
-    total_seqs,
-    keep_ref,
-    core_ref,
-    chip_ref,
-    relay_ref,
-    out_bias,
-    gate_weight,
-    up_weight,
-    down_weight,
-    bins_weight,
-    bins_bias,
-    symmetric_out,
-    bins_out,
-):
-    _, depth_count, sub_count = dims
-    pair_channels = gate_weight.shape[0]
-    bins = bins_weight.shape[0]
-    count = keep_ref.shape[0] // 2
-    piece = count // len(block_tiles)
-    band = piece * sub_count
-    tile, sub = lax.axis_index("tile"), lax.axis_index("sub")
-    if depth_count > 1:
-        here = keep_ref[...] + relay_ref[: 2 * count, :]
-        there = core_ref[...] + chip_ref[2 * count :, :]
-    else:
-        here, there = keep_ref[...], core_ref[...]
-    summed = jnp.concatenate([here[:count], there[:count], here[count:], there[count:]], axis=0)
+def half_row(total_seqs, summed, out_bias, gate_weight, up_weight, down_weight, bins_weight, bins_bias):
+    count = summed.shape[0] // 2
     pair = (summed * (1.0 / total_seqs) + out_bias[...]).astype(jnp.bfloat16)
     values = pair.astype(jnp.float32)
     center = jnp.mean(values, axis=-1, keepdims=True)
@@ -228,18 +191,38 @@
     hidden = (jax.nn.silu(gate) * up).astype(jnp.bfloat16)
     moved = (values + jnp.dot(hidden, down_weight[...], preferred_element_type=jnp.float32)).astype(jnp.bfloat16)
     moved = moved.astype(jnp.float32)
-    symmetric = ((moved[: 2 * count] + moved[2 * count :]) * 0.5).astype(jnp.bfloat16)
-    packed = LANES // bins
+    symmetric = ((moved[:count] + moved[count:]) * 0.5).astype(jnp.bfloat16)
+    packed = LANES // bins_weight.shape[0]
     weight = jnp.concatenate([bins_weight[...]] * packed, axis=0)
     bias = jnp.concatenate([bins_bias[...]] * packed, axis=1)
     logits = lax.dot_general(symmetric, weight, NT, preferred_element_type=jnp.float32) + bias
+    return symmetric.astype(jnp.float32), logits
+
+
+def there_kernel(total_seqs, depth_count, core_ref, chip_ref, *refs):
+    params, (symmetric_out, logits_out) = refs[:-2], refs[-2:]
+    summed = core_ref[...]
+    if depth_count > 1:
+        summed = summed + chip_ref[summed.shape[0] :, :]
+    symmetric_out[...], logits_out[...] = half_row(total_seqs, summed, *params)
+
+
+def here_kernel(dims, block_tiles, total_seqs, keep_ref, relay_ref, symmetric_there, logits_there, *refs):
+    _, depth_count, sub_count = dims
+    params, (symmetric_out, bins_out) = refs[:-2], refs[-2:]
+    count, pair_channels = symmetric_there.shape
+    bins = params[-2].shape[0]
+    piece = count // len(block_tiles)
+    band = piece * sub_count
+    packed = LANES // bins
+    tile, sub = lax.axis_index("tile"), lax.axis_index("sub")
     lane = lax.broadcasted_iota(jnp.int32, (1, LANES), 1)
-    symmetric = symmetric.astype(jnp.float32)
-    for side in range(2):
+
+    def write(side, symmetric, logits):
         for k, bits in enumerate(block_tiles):
             half = sub ^ (parity(bits) ^ side)
             start = (tile ^ bits) * band + half * piece
-            row = side * count + k * piece
+            row = k * piece
             for j in range(piece):
                 at = pl.multiple_of((start + j) * pair_channels, pair_channels)
                 symmetric_out[:, pl.ds(at, pair_channels)] = symmetric[row + j : row + j + 1].astype(jnp.bfloat16)
@@ -249,6 +232,12 @@
                     line = jnp.where(lane < p * bins, line, logits[row + j + p : row + j + p + 1])
                 at = pl.multiple_of((start + j) * bins, LANES)
                 bins_out[:, pl.ds(at, LANES)] = line
+
+    write(1, symmetric_there[...], logits_there[...])
+    summed = keep_ref[...]
+    if depth_count > 1:
+        summed = summed + relay_ref[...]
+    write(0, *half_row(total_seqs, summed, *params))
 
 
 def call(kernel, flops, outs, scratch, operands, sources=()):
@@ -293,7 +282,7 @@
     residues = residue_mask.shape[0]
     pair_channels = out_weight.shape[1]
     bins = distogram_weight.shape[1]
-    if channels * fold != LANES or band % fold or sub_count != 2 or band != depth_count * sub_count or tile_count & (tile_count - 1) or band & (band - 1):
+    if channels * fold != LANES or piece * bins % LANES or sub_count != 2 or band != depth_count * sub_count or tile_count & (tile_count - 1) or band & (band - 1):
         raise ValueError("unsupported mesh")
     dims = (channels, depth_count, sub_count)
     bf16, f32 = jnp.bfloat16, jnp.float32
@@ -371,18 +360,20 @@
     from_chip = xor_permute(chip, 0, 1, 1) if depth_count > 1 else chip
     from_core = xor_permute(core, 0, 0, 1)
     relayed = xor_permute(from_chip[: 2 * count], 0, 0, 1) if depth_count > 1 else from_core
+    total_seqs = seqs * depth_count
+    there = call(
+        functools.partial(there_kernel, total_seqs, depth_count),
+        1 << 24,
+        (shape(count, pair_channels, f32), shape(count, LANES, f32)),
+        [],
+        (from_core, from_chip, *params),
+    )
     return call(
-        functools.partial(finish_kernel, dims, block_tiles, seqs * depth_count),
-        1 << 25,
+        functools.partial(here_kernel, dims, block_tiles, total_seqs),
+        1 << 24,
         (shape(1, residues * pair_channels, bf16), shape(1, residues * bins, f32)),
         [],
-        (
-            keep,
-            from_core,
-            from_chip,
-            relayed,
-            *params,
-        ),
+        (keep, relayed, *there, *params),
     )
 
 

time: 17.8 us -> 17.6 us (0.989)
  waiting for transfers between devices: 3.5 us -> 2.97 us
  Pallas kernels: 3.91 us -> 4.33 us
    ppermute x7, waiting for transfers between devices: 3.5 us -> 2.97 us  [xor_permute(): return lax.ppermute(value, GROUP, pairs)]
    pallas_call x4 -> x5, Pallas kernels: 3.91 us -> 4.33 us  [call(): pl.pallas_call(kernel, out_shape=outs, in_specs=[VMEM] * len(operands) +...]
  transfers between devices with their start and end apart: 7 -> 7, of which waited for: 3 -> 3; matrix products, arithmetic and copies ran while one was open for 0% -> 0% of each run, Pallas kernels for 7% -> 11%
where the time goes in v5:
time: 17.6 us; the launch traced here: 17.4 us
  starting transfers between devices  9.45 us (54%)
  Pallas kernels  4.33 us (25%)
  waiting for transfers between devices  2.97 us (17%)
  between operations  0.67 us (4%)
    ppermute x7, starting transfers between devices, xor_permute(): return lax.ppermute(value, GROUP, pairs)  9.45 us
    pallas_call x5, Pallas kernels, call(): pl.pallas_call(kernel, out_shape=outs, in_specs=[VMEM] * len(operands) +...  4.33 us
    ppermute x7, waiting for transfers between devices, xor_permute(): return lax.ppermute(value, GROUP, pairs)  2.97 us
  transfers between devices with their start and end apart: 7, of which 3 were waited for; matrix products, arithmetic and copies ran while one was open for 0% of the time, Pallas kernels for 11%

profile of v5, /device:TPU:0, one launch (start us, length us, event | category | flops | bytes accessed | tf_op | source)
XLA Modules:
  0.0 17.4 jit_solution(2603587931437593635)
XLA Ops:
  0.6 1.0 %shard_map.131 = (bf16[128,128]{1,0:T(8,128)(2,1)S(1)}, bf16[128,128]{1,0:T(8,128)(2,1)S(1)}, bf16[64,128]{1,0:T(8,128)(2,1)S(1)}) custom-call(bf16[128,128]{1,0:T(8,128)(2,1)} %refs_0_.1, s32[4,128]{1,0:T(4,128)} %bitcast.8, bf16[64,128]{1,0:T(8,128)(2,1)} %bitcast.6, s32[2,128]{1,0:T(2,128)} %bitcast.9, s32[16]{0:T(128)} %refs_4_.1), custom_call_target="tpu_custom_call" | custom-call | flops 65536 | bytes 199680 | tf_op jit(solution)/shard_map/pallas_call | solution.py:247
  1.6 3.6 %collective-permute-start = (bf16[128,128]{1,0:T(8,128)(2,1)S(1)}, bf16[128,128]{1,0:T(8,128)(2,1)S(1)}, u32[]{:S(2)}, u32[]{:S(2)}) collective-permute-start(bf16[128,128]{1,0:T(8,128)(2,1)S(1)} %get-tuple-element.19.refs_0_), channel_id=1, source_target_pairs={{0,9},{1,8},{2,11},{3,10},{4,13},{5,12},{6,15},{7,14},{8,1},{9,0},... | collective-permute-start | bytes 98312 | tf_op jit(solution)/shard_map/ppermute | solution.py:33
  5.2 1.9 %collective-permute-start.2 = (bf16[128,128]{1,0:T(8,128)(2,1)S(1)}, bf16[128,128]{1,0:T(8,128)(2,1)S(1)}, u32[]{:S(2)}, u32[]{:S(2)}) collective-permute-start(bf16[128,128]{1,0:T(8,128)(2,1)S(1)} %get-tuple-element.19.refs_0_), channel_id=1, source_target_pairs={{0,5},{1,4},{2,7},{3,6},{4,1},{5,0},{6,3},{7,2},{8,13},{9,12},{10,... | collective-permute-start | bytes 98312 | tf_op jit(solution)/shard_map/ppermute | solution.py:33
  7.0 0.0 collective-permute-done.refs_1_
  7.0 1.9 %collective-permute-start.1 = (bf16[128,128]{1,0:T(8,128)(2,1)S(1)}, bf16[128,128]{1,0:T(8,128)(2,1)S(1)}, u32[]{:S(2)}, u32[]{:S(2)}) collective-permute-start(bf16[128,128]{1,0:T(8,128)(2,1)S(1)} %collective-permute-done.refs_1_), channel_id=1, source_target_pairs={{0,5},{1,4},{2,7},{3,6},{4,1},{5,0},{6,3},{7,2},{8,13},{9,12},{10,... | collective-permute-start | bytes 98312 | tf_op jit(solution)/shard_map/ppermute | solution.py:33
  9.0 0.2 %collective-permute-start.3 = (bf16[64,128]{1,0:T(8,128)(2,1)S(1)}, bf16[64,128]{1,0:T(8,128)(2,1)S(1)}, u32[]{:S(2)}, u32[]{:S(2)}) collective-permute-start(bf16[64,128]{1,0:T(8,128)(2,1)S(1)} %get-tuple-element.21.refs_4_), channel_id=1, source_target_pairs={{0,1},{1,0},{2,3},{3,2},{4,5},{5,4},{6,7},{7,6},{8,9},{9,8},{10,11... | collective-permute-start | bytes 49160 | tf_op jit(solution)/shard_map/ppermute | solution.py:33
  9.2 1.0 %collective-permute-done.3.refs_5_ = bf16[64,128]{1,0:T(8,128)(2,1)S(1)} collective-permute-done((bf16[64,128]{1,0:T(8,128)(2,1)S(1)}, bf16[64,128]{1,0:T(8,128)(2,1)S(1)}, u32[]{:S(2)}, u32[]{:S(2)}) %collective-permute-start.3) | collective-permute-done | bytes 16416 | tf_op jit(solution)/shard_map/ppermute | solution.py:33
  10.2 0.0 collective-permute-done.2.refs_2_
  10.2 1.3 %shard_map.132 = (f32[64,128]{1,0:T(8,128)S(1)}, bf16[128,128]{1,0:T(8,128)(2,1)S(1)}, bf16[1024,128]{1,0:T(8,128)(2,1)S(1)}, f32[1,128]{1,0:T(1,128)S(1)}, bf16...) custom-call(bf16[128,128]{1,0:T(8,128)(2,1)S(1)} %get-tuple-element., ...), custom_call_target="tpu_custom_call" | custom-call | flops 67108864 | bytes 1131264 | tf_op jit(solution)/shard_map/pallas_call | solution.py:247
  11.5 0.0 collective-permute-done.1.refs_0_
  11.5 0.4 %shard_map.133 = (f32[16,128]{1,0:T(8,128)S(1)}, f32[16,128]{1,0:T(8,128)S(1)}, f32[32,128]{1,0:T(8,128)S(1)}) custom-call(bf16[128,128]{1,0:T(8,128)(2,1)S(1)} %collective-permute-done.1.refs_0_, bf16[128,128]{1,0:T(8,128)(2,1)S(1)} %get-tuple-element.20.refs_3_.refs_1_, bf16[128,128]{1,0:T(8,128)(2,1)S(1)} %get-tuple-element.22.refs_2_, ...), custom_call_target="tpu_custom_call" | custom-call | flops 67108864 | bytes 491520 | tf_op jit(solution)/shard_map/pallas_call | solution.py:247
  11.9 1.4 %collective-permute-start.4 = (f32[32,128]{1,0:T(8,128)S(1)}, f32[32,128]{1,0:T(8,128)S(1)}, u32[]{:S(2)}, u32[]{:S(2)}) collective-permute-start(f32[32,128]{1,0:T(8,128)S(1)} %get-tuple-element.26), channel_id=1, source_target_pairs={{0,3},{1,2},{2,1},{3,0},{4,7},{5,6},{6,5},{7,4},{8,11},{9,10},{10,... | collective-permute-start | bytes 49160 | tf_op jit(solution)/shard_map/ppermute | solution.py:33
  13.2 0.3 %collective-permute-start.6 = (f32[16,128]{1,0:T(8,128)S(1)}, f32[16,128]{1,0:T(8,128)S(1)}, u32[]{:S(2)}, u32[]{:S(2)}) collective-permute-start(f32[16,128]{1,0:T(8,128)S(1)} %get-tuple-element.27), channel_id=1, source_target_pairs={{0,1},{1,0},{2,3},{3,2},{4,5},{5,4},{6,7},{7,6},{8,9},{9,8},{10,11... | collective-permute-start | bytes 24584 | tf_op jit(solution)/shard_map/ppermute | solution.py:33
  13.5 1.6 %collective-permute-done.4.chip_ref = f32[32,128]{1,0:T(8,128)S(1)} collective-permute-done((f32[32,128]{1,0:T(8,128)S(1)}, f32[32,128]{1,0:T(8,128)S(1)}, u32[]{:S(2)}, u32[]{:S(2)}) %collective-permute-start.4) | collective-permute-done | bytes 16416 | tf_op jit(solution)/shard_map/ppermute | solution.py:33
  15.1 0.2 %collective-permute-start.5 = (f32[16,128]{1,0:T(8,128)S(1)}, f32[16,128]{1,0:T(8,128)S(1)}, u32[]{:S(2)}, u32[]{:S(2)}) collective-permute-start(f32[16,128]{1,0:T(8,128)S(1)} %slice.4), channel_id=1, source_target_pairs={{0,1},{1,0},{2,3},{3,2},{4,5},{5,4},{6,7},{7,6},{8,9},{9,8},{10,11... | collective-permute-start | bytes 24584 | tf_op jit(solution)/shard_map/ppermute | solution.py:33
  15.3 0.0 collective-permute-done.6.core_ref
  15.3 0.5 %shard_map.134 = (f32[8,128]{1,0:T(8,128)S(1)}, f32[8,128]{1,0:T(8,128)S(1)}) custom-call(f32[16,128]{1,0:T(8,128)S(1)} %collective-permute-done.6.core_ref, f32[32,128]{1,0:T(8,128)S(1)} %collective-permute-done.4.chip_ref, f32[1,128]{1,0:T(1,128)S(1)} %get-tuple-element.28.refs_0_, bf16[128,512]{1,0:T(8,128)(2,1)S(1)} %get-tuple-element.29.refs_1_, ...), custom_call_target="tpu_custom_call" | custom-call | flops 16777216 | bytes 443136 | tf_op jit(solution)/shard_map/pallas_call | solution.py:247
  15.8 0.4 %collective-permute-done.5.relay_ref = f32[16,128]{1,0:T(8,128)S(1)} collective-permute-done((f32[16,128]{1,0:T(8,128)S(1)}, f32[16,128]{1,0:T(8,128)S(1)}, u32[]{:S(2)}, u32[]{:S(2)}) %collective-permute-start.5) | collective-permute-done | bytes 8224 | tf_op jit(solution)/shard_map/ppermute | solution.py:33
  16.3 1.2 %shard_map.135 = (bf16[1,2048]{1,0:T(2,128)(2,1)}, f32[1,1024]{1,0:T(1,128)}) custom-call(f32[16,128]{1,0:T(8,128)S(1)} %get-tuple-element.25.keep_ref, f32[16,128]{1,0:T(8,128)S(1)} %collective-permute-done.5.relay_ref, f32[8,128]{1,0:T(8,128)S(1)} %get-tuple-element.34.symmetric_there, f32[8,128]{1,0:T(8,128)S(1)} %get-tuple-element.35.logits_there, ...), custom_call_target="tpu_custom_call" | custom-call | flops 16777216 | bytes 443136 | tf_op jit(solution)/shard_map/pallas_call | solution.py:247
  (1 shorter events, 0.0 us)
Async XLA Ops:
  1.6 5.4 %collective-permute-start = (bf16[128,128]{1,0:T(8,128)(2,1)S(1)}, bf16[128,128]{1,0:T(8,128)(2,1)S(1)}, u32[]{:S(2)}, u32[]{:S(2)}) collective-permute-start(bf16[128,128]{1,0:T(8,128)(2,1)S(1)} %get-tuple-element.19.refs_0_), channel_id=1, source_target_pairs={{0,9},{1,8},{2,11},{3,10},{4,13},{5,12},{6,15},{7,14},{8,1},{9,0},... | collective-permute-start | bytes 98312 | tf_op jit(solution)/shard_map/ppermute | solution.py:33
  5.2 5.0 %collective-permute-start.2 = (bf16[128,128]{1,0:T(8,128)(2,1)S(1)}, bf16[128,128]{1,0:T(8,128)(2,1)S(1)}, u32[]{:S(2)}, u32[]{:S(2)}) collective-permute-start(bf16[128,128]{1,0:T(8,128)(2,1)S(1)} %get-tuple-element.19.refs_0_), channel_id=1, source_target_pairs={{0,5},{1,4},{2,7},{3,6},{4,1},{5,0},{6,3},{7,2},{8,13},{9,12},{10,... | collective-permute-start | bytes 98312 | tf_op jit(solution)/shard_map/ppermute | solution.py:33
  7.0 4.4 %collective-permute-start.1 = (bf16[128,128]{1,0:T(8,128)(2,1)S(1)}, bf16[128,128]{1,0:T(8,128)(2,1)S(1)}, u32[]{:S(2)}, u32[]{:S(2)}) collective-permute-start(bf16[128,128]{1,0:T(8,128)(2,1)S(1)} %collective-permute-done.refs_1_), channel_id=1, source_target_pairs={{0,5},{1,4},{2,7},{3,6},{4,1},{5,0},{6,3},{7,2},{8,13},{9,12},{10,... | collective-permute-start | bytes 98312 | tf_op jit(solution)/shard_map/ppermute | solution.py:33
  9.0 1.2 %collective-permute-start.3 = (bf16[64,128]{1,0:T(8,128)(2,1)S(1)}, bf16[64,128]{1,0:T(8,128)(2,1)S(1)}, u32[]{:S(2)}, u32[]{:S(2)}) collective-permute-start(bf16[64,128]{1,0:T(8,128)(2,1)S(1)} %get-tuple-element.21.refs_4_), channel_id=1, source_target_pairs={{0,1},{1,0},{2,3},{3,2},{4,5},{5,4},{6,7},{7,6},{8,9},{9,8},{10,11... | collective-permute-start | bytes 49160 | tf_op jit(solution)/shard_map/ppermute | solution.py:33
  11.9 3.2 %collective-permute-start.4 = (f32[32,128]{1,0:T(8,128)S(1)}, f32[32,128]{1,0:T(8,128)S(1)}, u32[]{:S(2)}, u32[]{:S(2)}) collective-permute-start(f32[32,128]{1,0:T(8,128)S(1)} %get-tuple-element.26), channel_id=1, source_target_pairs={{0,3},{1,2},{2,1},{3,0},{4,7},{5,6},{6,5},{7,4},{8,11},{9,10},{10,... | collective-permute-start | bytes 49160 | tf_op jit(solution)/shard_map/ppermute | solution.py:33
  13.2 2.1 %collective-permute-start.6 = (f32[16,128]{1,0:T(8,128)S(1)}, f32[16,128]{1,0:T(8,128)S(1)}, u32[]{:S(2)}, u32[]{:S(2)}) collective-permute-start(f32[16,128]{1,0:T(8,128)S(1)} %get-tuple-element.27), channel_id=1, source_target_pairs={{0,1},{1,0},{2,3},{3,2},{4,5},{5,4},{6,7},{7,6},{8,9},{9,8},{10,11... | collective-permute-start | bytes 24584 | tf_op jit(solution)/shard_map/ppermute | solution.py:33
  15.1 1.2 %collective-permute-start.5 = (f32[16,128]{1,0:T(8,128)S(1)}, f32[16,128]{1,0:T(8,128)S(1)}, u32[]{:S(2)}, u32[]{:S(2)}) collective-permute-start(f32[16,128]{1,0:T(8,128)S(1)} %slice.4), channel_id=1, source_target_pairs={{0,1},{1,0},{2,3},{3,2},{4,5},{5,4},{6,7},{7,6},{8,9},{9,8},{10,11... | collective-permute-start | bytes 24584 | tf_op jit(solution)/shard_map/ppermute | solution.py:33

commit v6 on v5

--- a/solution.py
+++ b/solution.py
@@ -51,41 +51,29 @@
     return copies
 
 
-def prepare_kernel(dims, *refs):
-    channels, _, sub_count = dims
-    sources, (block_ref, left_out, right_out), scratch = refs[:5], refs[5:8], refs[8:]
-    left_ref, left_exp_ref, right_ref, right_exp_ref, mask_ref, left_f32, semaphores = scratch
+def prepare_kernel(*refs):
+    sources, block_ref, scratch = refs[:5], refs[5], refs[6:]
+    left_ref, left_exp_ref, right_ref, right_exp_ref, mask_ref, turned, semaphores = scratch
     for copy in fetch(sources, scratch, semaphores):
         copy.wait()
     band = left_exp_ref.shape[0]
     piece = right_exp_ref.shape[0]
-    fold = channels // ROWS
-    tile, sub = lax.axis_index("tile"), lax.axis_index("sub")
-    mine = row_in_tile(sub_count)
-    half = fold * piece * ROWS
-    right = right_ref[...].astype(jnp.float32)
-    right_scale = jnp.exp2(right_exp_ref[...].astype(jnp.float32))
-    first = tile * band + sub * piece
+    channels = right_ref.shape[0] // piece
+    sub = lax.axis_index("sub")
+    first = lax.axis_index("tile") * band + sub * piece
+    turned[...] = jnp.transpose(left_ref[...])
     for j in range(piece):
-        scale = right_scale[j : j + 1] * mask_ref[first + j].astype(jnp.float32)
-        scaled = (right[j * channels : (j + 1) * channels] * scale).astype(jnp.bfloat16)
-        right_out[j * channels : (j + 1) * channels, :] = scaled
-        block_ref[half + j * channels : half + (j + 1) * channels, :] = scaled
-    left = jnp.transpose(left_ref[...].astype(jnp.float32))
-    left_scale = jnp.exp2(left_exp_ref[...].astype(jnp.float32))
-    for i in range(band):
-        scale = left_scale[i : i + 1] * mask_ref[tile * band + i].astype(jnp.float32)
-        left_f32[i * channels : (i + 1) * channels, :] = left[i * channels : (i + 1) * channels] * scale
-    for target, places in (
-        (block_ref, [sub * piece + j for j in range(piece)]),
-        (left_out, [mine ^ i for i in range(band)]),
-    ):
-        for x in range(fold):
-            rows = [
-                left_f32[pl.ds(pl.multiple_of(place * channels + x * ROWS, ROWS), ROWS), :] for place in places
-            ]
-            at = x * len(places) * ROWS
-            target[at : at + len(places) * ROWS, :] = jnp.concatenate(rows, axis=0).astype(jnp.bfloat16)
+        keep = mask_ref[first + j].astype(jnp.float32)
+        scale = jnp.exp2(right_exp_ref[j : j + 1].astype(jnp.float32)) * keep
+        right = right_ref[j * channels : (j + 1) * channels].astype(jnp.float32) * scale
+        block_ref[(piece + j) * channels : (piece + j + 1) * channels, :] = right.astype(jnp.bfloat16)
+        place = sub * piece + j
+        scale = jnp.exp2(left_exp_ref[pl.ds(place, 1), :].astype(jnp.float32)) * keep
+        rows = turned[pl.ds(pl.multiple_of(place * channels, channels), channels), :]
+        left = (rows.astype(jnp.float32) * scale).astype(jnp.bfloat16)
+        for x in range(channels // ROWS):
+            at = (x * piece + j) * ROWS
+            block_ref[at : at + ROWS, :] = left[x * ROWS : (x + 1) * ROWS]
 
 
 def pair_terms(channels, blocks, left_ref, right_ref, weight_ref, scratch, store, ready):
@@ -137,26 +125,33 @@
 
 def early_kernel(dims, block_count, total, *refs):
     channels, _, sub_count = dims
-    blocks, (left_ref, right_ref, other_ref), refs = refs[:block_count], refs[block_count:][:3], refs[block_count + 3 :]
-    params = (len(refs) - 5) // 2
-    sources, (terms_out, right_out), refs = refs[:params], refs[params:][:2], refs[params + 2 :]
-    targets, (both, scratch, semaphores) = refs[:params], refs[params:]
+    blocks, other_ref, refs = refs[:block_count], refs[block_count], refs[block_count + 1 :]
+    params = (len(refs) - 7) // 2
+    sources, (terms_out, left_out, right_out), refs = refs[:params], refs[params:][:3], refs[params + 3 :]
+    targets, (left_both, right_both, scratch, semaphores) = refs[:params], refs[params:]
     copies = fetch(sources, targets, semaphores)
-    seqs = right_ref.shape[1]
-    piece = right_ref.shape[0] // channels
+    seqs = other_ref.shape[1]
+    fold = channels // ROWS
+    piece = other_ref.shape[0] // channels // 2
+    half = piece * channels
+    band = right_out.shape[0] // channels
     sub = lax.axis_index("sub")
     mine = row_in_tile(sub_count)
-    both[sub] = right_ref[...].reshape(piece, channels, seqs)
-    both[1 - sub] = other_ref[...].reshape(piece, channels, seqs)
-    for i in range(right_out.shape[0] // channels):
-        here = mine ^ i
-        right_out[i * channels : (i + 1) * channels, :] = both[here // piece, here % piece]
+    for place, block in ((sub, blocks[0]), (1 - sub, other_ref)):
+        left_both[place] = block[:half, :].reshape(fold, piece, ROWS, seqs)
+        right_both[place] = block[half:, :].reshape(piece, channels, seqs)
+    for i in range(band):
+        side, j = (mine ^ i) // piece, (mine ^ i) % piece
+        right_out[i * channels : (i + 1) * channels, :] = right_both[side, j]
+        for x in range(fold):
+            at = (x * band + i) * ROWS
+            left_out[at : at + ROWS, :] = left_both[side, x, j]
 
     def store(i, way, terms):
         at = (i * 2 + way) * total
         terms_out[at : at + terms.shape[0], :] = terms
 
-    pair_terms(channels, list(blocks), left_ref, right_out, targets[0], scratch, store, copies[0].wait)
+    pair_terms(channels, list(blocks), left_out, right_out, targets[0], scratch, store, copies[0].wait)
     for copy in copies[1:]:
         copy.wait()
 
@@ -288,18 +283,14 @@
     bf16, f32 = jnp.bfloat16, jnp.float32
 
     sources = (left_mantissa, left_exponent.T, right_mantissa.T, right_exponent.T, residue_mask)
-    own, left_rows, right_rows = call(
-        functools.partial(prepare_kernel, dims),
+    (own,) = call(
+        prepare_kernel,
         1 << 16,
-        (
-            shape(2 * piece * channels, seqs, bf16),
-            shape(band * channels, seqs, bf16),
-            shape(piece * channels, seqs, bf16),
-        ),
+        (shape(2 * piece * channels, seqs, bf16),),
         [pltpu.VMEM(s.shape, s.dtype) for s in sources[:4]]
         + [
             pltpu.SMEM(residue_mask.shape, residue_mask.dtype),
-            pltpu.VMEM((band * channels, seqs), f32),
+            pltpu.VMEM((width, seqs), bf16),
             pltpu.SemaphoreType.DMA((len(sources),)),
         ],
         (),
@@ -309,7 +300,7 @@
     for bit in bits_of(tile_count):
         for bits in list(blocks):
             blocks[bits ^ bit] = xor_permute(blocks[bits], bit, 0, 1)
-    other_rows = xor_permute(right_rows, 0, 0, 1)
+    other = xor_permute(own, 0, 0, 1)
     order = list(blocks)
     early, late = order[: max(len(order) * 3 // 4, 1)], order[max(len(order) * 3 // 4, 1) :]
     count = len(order) * piece
@@ -322,20 +313,22 @@
         distogram_weight.T,
         distogram_bias.reshape(1, -1),
     )
-    terms, right_rows, weight, *params = call(
+    terms, left_rows, right_rows, weight, *params = call(
         functools.partial(early_kernel, dims, len(early), count),
         1 << 26,
         (
             shape(band * 2 * count, pair_channels, f32),
             shape(band * channels, seqs, bf16),
+            shape(band * channels, seqs, bf16),
             *(shape(*p.shape, p.dtype) for p in params),
         ),
         [
+            pltpu.VMEM((sub_count, fold, piece, ROWS, seqs), bf16),
             pltpu.VMEM((sub_count, piece, channels, seqs), bf16),
             pltpu.VMEM((2 * band * len(early) * piece * ROWS, LANES), f32),
             pltpu.SemaphoreType.DMA((len(params),)),
         ],
-        (*(blocks[k] for k in early), left_rows, right_rows, other_rows),
+        (*(blocks[k] for k in early), other),
         params,
     )
     keep, core, chip = call(

time: 17.6 us -> 16.7 us (0.949)
  waiting for transfers between devices: 2.97 us -> 1.87 us
  starting transfers between devices: 9.45 us -> 9.66 us
    ppermute x7, waiting for transfers between devices: 2.97 us -> 1.87 us  [xor_permute(): return lax.ppermute(value, GROUP, pairs)]
    ppermute x7, starting transfers between devices: 9.45 us -> 9.66 us  [xor_permute(): return lax.ppermute(value, GROUP, pairs)]
where the time goes in v6:
time: 16.7 us; the launch traced here: 16.5 us
  starting transfers between devices  9.66 us (58%)
  Pallas kernels  4.3 us (26%)
  waiting for transfers between devices  1.87 us (11%)
  between operations  0.66 us (4%)
    ppermute x7, starting transfers between devices, xor_permute(): return lax.ppermute(value, GROUP, pairs)  9.66 us
    pallas_call x5, Pallas kernels, call(): pl.pallas_call(kernel, out_shape=outs, in_specs=[VMEM] * len(operands) +...  4.3 us
    ppermute x7, waiting for transfers between devices, xor_permute(): return lax.ppermute(value, GROUP, pairs)  1.87 us
  transfers between devices with their start and end apart: 7, of which 3 were waited for; matrix products, arithmetic and copies ran while one was open for 0% of the time, Pallas kernels for 11%

profile of v6, /device:TPU:0, one launch (start us, length us, event | category | flops | bytes accessed | tf_op | source)
XLA Modules:
  0.0 16.5 jit_solution(13250364607272737195)
XLA Ops:
  0.6 0.9 %shard_map.131.refs_0_ = bf16[128,128]{1,0:T(8,128)(2,1)S(1)} custom-call(bf16[128,128]{1,0:T(8,128)(2,1)} %refs_0_.1, s32[4,128]{1,0:T(4,128)} %bitcast.8, bf16[64,128]{1,0:T(8,128)(2,1)} %bitcast.7, s32[2,128]{1,0:T(2,128)} %bitcast.9, s32[16]{0:T(128)} %refs_4_.2), custom_call_target="tpu_custom_call" | custom-call | flops 65536 | bytes 117760 | tf_op jit(solution)/shard_map/pallas_call | solution.py:242
  1.6 3.6 %collective-permute-start = (bf16[128,128]{1,0:T(8,128)(2,1)S(1)}, bf16[128,128]{1,0:T(8,128)(2,1)S(1)}, u32[]{:S(2)}, u32[]{:S(2)}) collective-permute-start(bf16[128,128]{1,0:T(8,128)(2,1)S(1)} %shard_map.131.refs_0_), channel_id=1, source_target_pairs={{0,9},{1,8},{2,11},{3,10},{4,13},{5,12},{6,15},{7,14},{8,1},{9,0},... | collective-permute-start | bytes 98312 | tf_op jit(solution)/shard_map/ppermute | solution.py:33
  5.1 1.9 %collective-permute-start.2 = (bf16[128,128]{1,0:T(8,128)(2,1)S(1)}, bf16[128,128]{1,0:T(8,128)(2,1)S(1)}, u32[]{:S(2)}, u32[]{:S(2)}) collective-permute-start(bf16[128,128]{1,0:T(8,128)(2,1)S(1)} %shard_map.131.refs_0_), channel_id=1, source_target_pairs={{0,5},{1,4},{2,7},{3,6},{4,1},{5,0},{6,3},{7,2},{8,13},{9,12},{10,... | collective-permute-start | bytes 98312 | tf_op jit(solution)/shard_map/ppermute | solution.py:33
  7.0 0.0 collective-permute-start.3
  7.0 0.0 collective-permute-done.refs_1_
  7.0 1.9 %collective-permute-start.1 = (bf16[128,128]{1,0:T(8,128)(2,1)S(1)}, bf16[128,128]{1,0:T(8,128)(2,1)S(1)}, u32[]{:S(2)}, u32[]{:S(2)}) collective-permute-start(bf16[128,128]{1,0:T(8,128)(2,1)S(1)} %collective-permute-done.refs_1_), channel_id=1, source_target_pairs={{0,5},{1,4},{2,7},{3,6},{4,1},{5,0},{6,3},{7,2},{8,13},{9,12},{10,... | collective-permute-start | bytes 98312 | tf_op jit(solution)/shard_map/ppermute | solution.py:33
  8.9 0.0 collective-permute-done.2.refs_2_
  8.9 0.0 collective-permute-done.3.refs_3_
  8.9 1.3 %shard_map.132 = (f32[64,128]{1,0:T(8,128)S(1)}, bf16[128,128]{1,0:T(8,128)(2,1)S(1)}, bf16[128,128]{1,0:T(8,128)(2,1)S(1)}, bf16[1024,128]{1,0:T(8,128)(2,1)S(1...) custom-call(bf16[128,128]{1,0:T(8,128)(2,1)S(1)} %shard_map.131.refs, ...), custom_call_target="tpu_custom_call" | custom-call | flops 67108864 | bytes 1164032 | tf_op jit(solution)/shard_map/pallas_call | solution.py:242
  10.2 0.3 %collective-permute-done.1.refs_0_ = bf16[128,128]{1,0:T(8,128)(2,1)S(1)} collective-permute-done((bf16[128,128]{1,0:T(8,128)(2,1)S(1)}, bf16[128,128]{1,0:T(8,128)(2,1)S(1)}, u32[]{:S(2)}, u32[]{:S(2)}) %collective-permute-start.1) | collective-permute-done | bytes 32800 | tf_op jit(solution)/shard_map/ppermute | solution.py:33
  10.5 0.4 %shard_map.133 = (f32[16,128]{1,0:T(8,128)S(1)}, f32[16,128]{1,0:T(8,128)S(1)}, f32[32,128]{1,0:T(8,128)S(1)}) custom-call(bf16[128,128]{1,0:T(8,128)(2,1)S(1)} %collective-permute-done.1.refs_0_, bf16[128,128]{1,0:T(8,128)(2,1)S(1)} %get-tuple-element.17.refs_1_, bf16[128,128]{1,0:T(8,128)(2,1)S(1)} %get-tuple-element.18.refs_2_, ...), custom_call_target="tpu_custom_call" | custom-call | flops 67108864 | bytes 491520 | tf_op jit(solution)/shard_map/pallas_call | solution.py:242
  10.9 1.6 %collective-permute-start.4 = (f32[32,128]{1,0:T(8,128)S(1)}, f32[32,128]{1,0:T(8,128)S(1)}, u32[]{:S(2)}, u32[]{:S(2)}) collective-permute-start(f32[32,128]{1,0:T(8,128)S(1)} %get-tuple-element.22), channel_id=1, source_target_pairs={{0,3},{1,2},{2,1},{3,0},{4,7},{5,6},{6,5},{7,4},{8,11},{9,10},{10,... | collective-permute-start | bytes 49160 | tf_op jit(solution)/shard_map/ppermute | solution.py:33
  12.5 0.4 %collective-permute-start.6 = (f32[16,128]{1,0:T(8,128)S(1)}, f32[16,128]{1,0:T(8,128)S(1)}, u32[]{:S(2)}, u32[]{:S(2)}) collective-permute-start(f32[16,128]{1,0:T(8,128)S(1)} %get-tuple-element.23), channel_id=1, source_target_pairs={{0,1},{1,0},{2,3},{3,2},{4,5},{5,4},{6,7},{7,6},{8,9},{9,8},{10,11... | collective-permute-start | bytes 24584 | tf_op jit(solution)/shard_map/ppermute | solution.py:33
  12.9 1.2 %collective-permute-done.4.chip_ref = f32[32,128]{1,0:T(8,128)S(1)} collective-permute-done((f32[32,128]{1,0:T(8,128)S(1)}, f32[32,128]{1,0:T(8,128)S(1)}, u32[]{:S(2)}, u32[]{:S(2)}) %collective-permute-start.4) | collective-permute-done | bytes 16416 | tf_op jit(solution)/shard_map/ppermute | solution.py:33
  14.2 0.3 %collective-permute-start.5 = (f32[16,128]{1,0:T(8,128)S(1)}, f32[16,128]{1,0:T(8,128)S(1)}, u32[]{:S(2)}, u32[]{:S(2)}) collective-permute-start(f32[16,128]{1,0:T(8,128)S(1)} %slice.4), channel_id=1, source_target_pairs={{0,1},{1,0},{2,3},{3,2},{4,5},{5,4},{6,7},{7,6},{8,9},{9,8},{10,11... | collective-permute-start | bytes 24584 | tf_op jit(solution)/shard_map/ppermute | solution.py:33
  14.5 0.0 collective-permute-done.6.core_ref
  14.5 0.5 %shard_map.134 = (f32[8,128]{1,0:T(8,128)S(1)}, f32[8,128]{1,0:T(8,128)S(1)}) custom-call(f32[16,128]{1,0:T(8,128)S(1)} %collective-permute-done.6.core_ref, f32[32,128]{1,0:T(8,128)S(1)} %collective-permute-done.4.chip_ref, f32[1,128]{1,0:T(1,128)S(1)} %get-tuple-element.24.refs_0_, bf16[128,512]{1,0:T(8,128)(2,1)S(1)} %get-tuple-element.25.refs_1_, ...), custom_call_target="tpu_custom_call" | custom-call | flops 16777216 | bytes 443136 | tf_op jit(solution)/shard_map/pallas_call | solution.py:242
  15.0 0.3 %collective-permute-done.5.relay_ref = f32[16,128]{1,0:T(8,128)S(1)} collective-permute-done((f32[16,128]{1,0:T(8,128)S(1)}, f32[16,128]{1,0:T(8,128)S(1)}, u32[]{:S(2)}, u32[]{:S(2)}) %collective-permute-start.5) | collective-permute-done | bytes 8224 | tf_op jit(solution)/shard_map/ppermute | solution.py:33
  15.3 1.2 %shard_map.135 = (bf16[1,2048]{1,0:T(2,128)(2,1)}, f32[1,1024]{1,0:T(1,128)}) custom-call(f32[16,128]{1,0:T(8,128)S(1)} %get-tuple-element.21.keep_ref, f32[16,128]{1,0:T(8,128)S(1)} %collective-permute-done.5.relay_ref, f32[8,128]{1,0:T(8,128)S(1)} %get-tuple-element.30.symmetric_there, f32[8,128]{1,0:T(8,128)S(1)} %get-tuple-element.31.logits_there, ...), custom_call_target="tpu_custom_call" | custom-call | flops 16777216 | bytes 443136 | tf_op jit(solution)/shard_map/pallas_call | solution.py:242
  (1 shorter events, 0.0 us)
Async XLA Ops:
  1.6 5.4 %collective-permute-start = (bf16[128,128]{1,0:T(8,128)(2,1)S(1)}, bf16[128,128]{1,0:T(8,128)(2,1)S(1)}, u32[]{:S(2)}, u32[]{:S(2)}) collective-permute-start(bf16[128,128]{1,0:T(8,128)(2,1)S(1)} %shard_map.131.refs_0_), channel_id=1, source_target_pairs={{0,9},{1,8},{2,11},{3,10},{4,13},{5,12},{6,15},{7,14},{8,1},{9,0},... | collective-permute-start | bytes 98312 | tf_op jit(solution)/shard_map/ppermute | solution.py:33
  5.1 3.8 %collective-permute-start.2 = (bf16[128,128]{1,0:T(8,128)(2,1)S(1)}, bf16[128,128]{1,0:T(8,128)(2,1)S(1)}, u32[]{:S(2)}, u32[]{:S(2)}) collective-permute-start(bf16[128,128]{1,0:T(8,128)(2,1)S(1)} %shard_map.131.refs_0_), channel_id=1, source_target_pairs={{0,5},{1,4},{2,7},{3,6},{4,1},{5,0},{6,3},{7,2},{8,13},{9,12},{10,... | collective-permute-start | bytes 98312 | tf_op jit(solution)/shard_map/ppermute | solution.py:33
  7.0 2.0 %collective-permute-start.3 = (bf16[128,128]{1,0:T(8,128)(2,1)S(1)}, bf16[128,128]{1,0:T(8,128)(2,1)S(1)}, u32[]{:S(2)}, u32[]{:S(2)}) collective-permute-start(bf16[128,128]{1,0:T(8,128)(2,1)S(1)} %shard_map.131.refs_0_), channel_id=1, source_target_pairs={{0,1},{1,0},{2,3},{3,2},{4,5},{5,4},{6,7},{7,6},{8,9},{9,8},{10,11... | collective-permute-start | bytes 98312 | tf_op jit(solution)/shard_map/ppermute | solution.py:33
  7.0 3.5 %collective-permute-start.1 = (bf16[128,128]{1,0:T(8,128)(2,1)S(1)}, bf16[128,128]{1,0:T(8,128)(2,1)S(1)}, u32[]{:S(2)}, u32[]{:S(2)}) collective-permute-start(bf16[128,128]{1,0:T(8,128)(2,1)S(1)} %collective-permute-done.refs_1_), channel_id=1, source_target_pairs={{0,5},{1,4},{2,7},{3,6},{4,1},{5,0},{6,3},{7,2},{8,13},{9,12},{10,... | collective-permute-start | bytes 98312 | tf_op jit(solution)/shard_map/ppermute | solution.py:33
  10.9 3.2 %collective-permute-start.4 = (f32[32,128]{1,0:T(8,128)S(1)}, f32[32,128]{1,0:T(8,128)S(1)}, u32[]{:S(2)}, u32[]{:S(2)}) collective-permute-start(f32[32,128]{1,0:T(8,128)S(1)} %get-tuple-element.22), channel_id=1, source_target_pairs={{0,3},{1,2},{2,1},{3,0},{4,7},{5,6},{6,5},{7,4},{8,11},{9,10},{10,... | collective-permute-start | bytes 49160 | tf_op jit(solution)/shard_map/ppermute | solution.py:33
  12.5 2.0 %collective-permute-start.6 = (f32[16,128]{1,0:T(8,128)S(1)}, f32[16,128]{1,0:T(8,128)S(1)}, u32[]{:S(2)}, u32[]{:S(2)}) collective-permute-start(f32[16,128]{1,0:T(8,128)S(1)} %get-tuple-element.23), channel_id=1, source_target_pairs={{0,1},{1,0},{2,3},{3,2},{4,5},{5,4},{6,7},{7,6},{8,9},{9,8},{10,11... | collective-permute-start | bytes 24584 | tf_op jit(solution)/shard_map/ppermute | solution.py:33
  14.2 1.2 %collective-permute-start.5 = (f32[16,128]{1,0:T(8,128)S(1)}, f32[16,128]{1,0:T(8,128)S(1)}, u32[]{:S(2)}, u32[]{:S(2)}) collective-permute-start(f32[16,128]{1,0:T(8,128)S(1)} %slice.4), channel_id=1, source_target_pairs={{0,1},{1,0},{2,3},{3,2},{4,5},{5,4},{6,7},{7,6},{8,9},{9,8},{10,11... | collective-permute-start | bytes 24584 | tf_op jit(solution)/shard_map/ppermute | solution.py:33

commit v7 on v6

--- a/solution.py
+++ b/solution.py
@@ -42,8 +42,9 @@
 
 
 def fetch(sources, targets, semaphores):
+    last = semaphores.shape[0] - 1
     copies = [
-        pltpu.make_async_copy(source, target, semaphores.at[n])
+        pltpu.make_async_copy(source, target, semaphores.at[min(n, last)])
         for n, (source, target) in enumerate(zip(sources, targets))
     ]
     for copy in copies:
@@ -291,7 +292,7 @@
         + [
             pltpu.SMEM(residue_mask.shape, residue_mask.dtype),
             pltpu.VMEM((width, seqs), bf16),
-            pltpu.SemaphoreType.DMA((len(sources),)),
+            pltpu.SemaphoreType.DMA((1,)),
         ],
         (),
         sources,
@@ -326,7 +327,7 @@
             pltpu.VMEM((sub_count, fold, piece, ROWS, seqs), bf16),
             pltpu.VMEM((sub_count, piece, channels, seqs), bf16),
             pltpu.VMEM((2 * band * len(early) * piece * ROWS, LANES), f32),
-            pltpu.SemaphoreType.DMA((len(params),)),
+            pltpu.SemaphoreType.DMA((2,)),
         ],
         (*(blocks[k] for k in early), other),
         params,

time: 16.7 us -> 16.7 us (level)
  no operation moved by 1% of the time
where the time goes in v7:
time: 16.7 us; the launch traced here: 16.5 us
  starting transfers between devices  9.66 us (58%)
  Pallas kernels  4.21 us (25%)
  waiting for transfers between devices  1.92 us (11%)
  between operations  0.66 us (4%)
    ppermute x7, starting transfers between devices, xor_permute(): return lax.ppermute(value, GROUP, pairs)  9.66 us
    pallas_call x5, Pallas kernels, call(): pl.pallas_call(kernel, out_shape=outs, in_specs=[VMEM] * len(operands) +...  4.21 us
    ppermute x7, waiting for transfers between devices, xor_permute(): return lax.ppermute(value, GROUP, pairs)  1.92 us
  transfers between devices with their start and end apart: 7, of which 3 were waited for; matrix products, arithmetic and copies ran while one was open for 0% of the time, Pallas kernels for 11%

profile of v7, /device:TPU:0, one launch (start us, length us, event | category | flops | bytes accessed | tf_op | source)
XLA Modules:
  0.0 16.5 jit_solution(14273797365892577802)
XLA Ops:
  0.6 0.9 %shard_map.131.refs_0_ = bf16[128,128]{1,0:T(8,128)(2,1)S(1)} custom-call(bf16[128,128]{1,0:T(8,128)(2,1)} %refs_0_.1, s32[4,128]{1,0:T(4,128)} %bitcast.8, bf16[64,128]{1,0:T(8,128)(2,1)} %bitcast.7, s32[2,128]{1,0:T(2,128)} %bitcast.9, s32[16]{0:T(128)} %refs_4_.2), custom_call_target="tpu_custom_call" | custom-call | flops 65536 | bytes 117760 | tf_op jit(solution)/shard_map/pallas_call | solution.py:243
  1.5 3.6 %collective-permute-start = (bf16[128,128]{1,0:T(8,128)(2,1)S(1)}, bf16[128,128]{1,0:T(8,128)(2,1)S(1)}, u32[]{:S(2)}, u32[]{:S(2)}) collective-permute-start(bf16[128,128]{1,0:T(8,128)(2,1)S(1)} %shard_map.131.refs_0_), channel_id=1, source_target_pairs={{0,9},{1,8},{2,11},{3,10},{4,13},{5,12},{6,15},{7,14},{8,1},{9,0},... | collective-permute-start | bytes 98312 | tf_op jit(solution)/shard_map/ppermute | solution.py:33
  5.1 1.9 %collective-permute-start.2 = (bf16[128,128]{1,0:T(8,128)(2,1)S(1)}, bf16[128,128]{1,0:T(8,128)(2,1)S(1)}, u32[]{:S(2)}, u32[]{:S(2)}) collective-permute-start(bf16[128,128]{1,0:T(8,128)(2,1)S(1)} %shard_map.131.refs_0_), channel_id=1, source_target_pairs={{0,5},{1,4},{2,7},{3,6},{4,1},{5,0},{6,3},{7,2},{8,13},{9,12},{10,... | collective-permute-start | bytes 98312 | tf_op jit(solution)/shard_map/ppermute | solution.py:33
  7.0 0.0 collective-permute-start.3
  7.0 0.0 collective-permute-done.refs_1_
  7.0 1.9 %collective-permute-start.1 = (bf16[128,128]{1,0:T(8,128)(2,1)S(1)}, bf16[128,128]{1,0:T(8,128)(2,1)S(1)}, u32[]{:S(2)}, u32[]{:S(2)}) collective-permute-start(bf16[128,128]{1,0:T(8,128)(2,1)S(1)} %collective-permute-done.refs_1_), channel_id=1, source_target_pairs={{0,5},{1,4},{2,7},{3,6},{4,1},{5,0},{6,3},{7,2},{8,13},{9,12},{10,... | collective-permute-start | bytes 98312 | tf_op jit(solution)/shard_map/ppermute | solution.py:33
  8.9 0.0 collective-permute-done.2.refs_2_
  8.9 0.0 collective-permute-done.3.refs_3_
  8.9 1.2 %shard_map.132 = (f32[64,128]{1,0:T(8,128)S(1)}, bf16[128,128]{1,0:T(8,128)(2,1)S(1)}, bf16[128,128]{1,0:T(8,128)(2,1)S(1)}, bf16[1024,128]{1,0:T(8,128)(2,1)S(1...) custom-call(bf16[128,128]{1,0:T(8,128)(2,1)S(1)} %shard_map.131.refs, ...), custom_call_target="tpu_custom_call" | custom-call | flops 67108864 | bytes 1164032 | tf_op jit(solution)/shard_map/pallas_call | solution.py:243
  10.2 0.3 %collective-permute-done.1.refs_0_ = bf16[128,128]{1,0:T(8,128)(2,1)S(1)} collective-permute-done((bf16[128,128]{1,0:T(8,128)(2,1)S(1)}, bf16[128,128]{1,0:T(8,128)(2,1)S(1)}, u32[]{:S(2)}, u32[]{:S(2)}) %collective-permute-start.1) | collective-permute-done | bytes 32800 | tf_op jit(solution)/shard_map/ppermute | solution.py:33
  10.5 0.4 %shard_map.133 = (f32[16,128]{1,0:T(8,128)S(1)}, f32[16,128]{1,0:T(8,128)S(1)}, f32[32,128]{1,0:T(8,128)S(1)}) custom-call(bf16[128,128]{1,0:T(8,128)(2,1)S(1)} %collective-permute-done.1.refs_0_, bf16[128,128]{1,0:T(8,128)(2,1)S(1)} %get-tuple-element.17.refs_1_, bf16[128,128]{1,0:T(8,128)(2,1)S(1)} %get-tuple-element.18.refs_2_, ...), custom_call_target="tpu_custom_call" | custom-call | flops 67108864 | bytes 491520 | tf_op jit(solution)/shard_map/pallas_call | solution.py:243
  10.9 1.6 %collective-permute-start.4 = (f32[32,128]{1,0:T(8,128)S(1)}, f32[32,128]{1,0:T(8,128)S(1)}, u32[]{:S(2)}, u32[]{:S(2)}) collective-permute-start(f32[32,128]{1,0:T(8,128)S(1)} %get-tuple-element.22), channel_id=1, source_target_pairs={{0,3},{1,2},{2,1},{3,0},{4,7},{5,6},{6,5},{7,4},{8,11},{9,10},{10,... | collective-permute-start | bytes 49160 | tf_op jit(solution)/shard_map/ppermute | solution.py:33
  12.5 0.4 %collective-permute-start.6 = (f32[16,128]{1,0:T(8,128)S(1)}, f32[16,128]{1,0:T(8,128)S(1)}, u32[]{:S(2)}, u32[]{:S(2)}) collective-permute-start(f32[16,128]{1,0:T(8,128)S(1)} %get-tuple-element.23), channel_id=1, source_target_pairs={{0,1},{1,0},{2,3},{3,2},{4,5},{5,4},{6,7},{7,6},{8,9},{9,8},{10,11... | collective-permute-start | bytes 24584 | tf_op jit(solution)/shard_map/ppermute | solution.py:33
  12.9 1.2 %collective-permute-done.4.chip_ref = f32[32,128]{1,0:T(8,128)S(1)} collective-permute-done((f32[32,128]{1,0:T(8,128)S(1)}, f32[32,128]{1,0:T(8,128)S(1)}, u32[]{:S(2)}, u32[]{:S(2)}) %collective-permute-start.4) | collective-permute-done | bytes 16416 | tf_op jit(solution)/shard_map/ppermute | solution.py:33
  14.1 0.3 %collective-permute-start.5 = (f32[16,128]{1,0:T(8,128)S(1)}, f32[16,128]{1,0:T(8,128)S(1)}, u32[]{:S(2)}, u32[]{:S(2)}) collective-permute-start(f32[16,128]{1,0:T(8,128)S(1)} %slice.4), channel_id=1, source_target_pairs={{0,1},{1,0},{2,3},{3,2},{4,5},{5,4},{6,7},{7,6},{8,9},{9,8},{10,11... | collective-permute-start | bytes 24584 | tf_op jit(solution)/shard_map/ppermute | solution.py:33
  14.4 0.0 collective-permute-done.6.core_ref
  14.4 0.5 %shard_map.134 = (f32[8,128]{1,0:T(8,128)S(1)}, f32[8,128]{1,0:T(8,128)S(1)}) custom-call(f32[16,128]{1,0:T(8,128)S(1)} %collective-permute-done.6.core_ref, f32[32,128]{1,0:T(8,128)S(1)} %collective-permute-done.4.chip_ref, f32[1,128]{1,0:T(1,128)S(1)} %get-tuple-element.24.refs_0_, bf16[128,512]{1,0:T(8,128)(2,1)S(1)} %get-tuple-element.25.refs_1_, ...), custom_call_target="tpu_custom_call" | custom-call | flops 16777216 | bytes 443136 | tf_op jit(solution)/shard_map/pallas_call | solution.py:243
  15.0 0.3 %collective-permute-done.5.relay_ref = f32[16,128]{1,0:T(8,128)S(1)} collective-permute-done((f32[16,128]{1,0:T(8,128)S(1)}, f32[16,128]{1,0:T(8,128)S(1)}, u32[]{:S(2)}, u32[]{:S(2)}) %collective-permute-start.5) | collective-permute-done | bytes 8224 | tf_op jit(solution)/shard_map/ppermute | solution.py:33
  15.3 1.2 %shard_map.135 = (bf16[1,2048]{1,0:T(2,128)(2,1)}, f32[1,1024]{1,0:T(1,128)}) custom-call(f32[16,128]{1,0:T(8,128)S(1)} %get-tuple-element.21.keep_ref, f32[16,128]{1,0:T(8,128)S(1)} %collective-permute-done.5.relay_ref, f32[8,128]{1,0:T(8,128)S(1)} %get-tuple-element.30.symmetric_there, f32[8,128]{1,0:T(8,128)S(1)} %get-tuple-element.31.logits_there, ...), custom_call_target="tpu_custom_call" | custom-call | flops 16777216 | bytes 443136 | tf_op jit(solution)/shard_map/pallas_call | solution.py:243
  (1 shorter events, 0.0 us)
Async XLA Ops:
  1.5 5.4 %collective-permute-start = (bf16[128,128]{1,0:T(8,128)(2,1)S(1)}, bf16[128,128]{1,0:T(8,128)(2,1)S(1)}, u32[]{:S(2)}, u32[]{:S(2)}) collective-permute-start(bf16[128,128]{1,0:T(8,128)(2,1)S(1)} %shard_map.131.refs_0_), channel_id=1, source_target_pairs={{0,9},{1,8},{2,11},{3,10},{4,13},{5,12},{6,15},{7,14},{8,1},{9,0},... | collective-permute-start | bytes 98312 | tf_op jit(solution)/shard_map/ppermute | solution.py:33
  5.1 3.8 %collective-permute-start.2 = (bf16[128,128]{1,0:T(8,128)(2,1)S(1)}, bf16[128,128]{1,0:T(8,128)(2,1)S(1)}, u32[]{:S(2)}, u32[]{:S(2)}) collective-permute-start(bf16[128,128]{1,0:T(8,128)(2,1)S(1)} %shard_map.131.refs_0_), channel_id=1, source_target_pairs={{0,5},{1,4},{2,7},{3,6},{4,1},{5,0},{6,3},{7,2},{8,13},{9,12},{10,... | collective-permute-start | bytes 98312 | tf_op jit(solution)/shard_map/ppermute | solution.py:33
  7.0 2.0 %collective-permute-start.3 = (bf16[128,128]{1,0:T(8,128)(2,1)S(1)}, bf16[128,128]{1,0:T(8,128)(2,1)S(1)}, u32[]{:S(2)}, u32[]{:S(2)}) collective-permute-start(bf16[128,128]{1,0:T(8,128)(2,1)S(1)} %shard_map.131.refs_0_), channel_id=1, source_target_pairs={{0,1},{1,0},{2,3},{3,2},{4,5},{5,4},{6,7},{7,6},{8,9},{9,8},{10,11... | collective-permute-start | bytes 98312 | tf_op jit(solution)/shard_map/ppermute | solution.py:33
  7.0 3.5 %collective-permute-start.1 = (bf16[128,128]{1,0:T(8,128)(2,1)S(1)}, bf16[128,128]{1,0:T(8,128)(2,1)S(1)}, u32[]{:S(2)}, u32[]{:S(2)}) collective-permute-start(bf16[128,128]{1,0:T(8,128)(2,1)S(1)} %collective-permute-done.refs_1_), channel_id=1, source_target_pairs={{0,5},{1,4},{2,7},{3,6},{4,1},{5,0},{6,3},{7,2},{8,13},{9,12},{10,... | collective-permute-start | bytes 98312 | tf_op jit(solution)/shard_map/ppermute | solution.py:33
  10.9 3.2 %collective-permute-start.4 = (f32[32,128]{1,0:T(8,128)S(1)}, f32[32,128]{1,0:T(8,128)S(1)}, u32[]{:S(2)}, u32[]{:S(2)}) collective-permute-start(f32[32,128]{1,0:T(8,128)S(1)} %get-tuple-element.22), channel_id=1, source_target_pairs={{0,3},{1,2},{2,1},{3,0},{4,7},{5,6},{6,5},{7,4},{8,11},{9,10},{10,... | collective-permute-start | bytes 49160 | tf_op jit(solution)/shard_map/ppermute | solution.py:33
  12.5 2.0 %collective-permute-start.6 = (f32[16,128]{1,0:T(8,128)S(1)}, f32[16,128]{1,0:T(8,128)S(1)}, u32[]{:S(2)}, u32[]{:S(2)}) collective-permute-start(f32[16,128]{1,0:T(8,128)S(1)} %get-tuple-element.23), channel_id=1, source_target_pairs={{0,1},{1,0},{2,3},{3,2},{4,5},{5,4},{6,7},{7,6},{8,9},{9,8},{10,11... | collective-permute-start | bytes 24584 | tf_op jit(solution)/shard_map/ppermute | solution.py:33
  14.1 1.2 %collective-permute-start.5 = (f32[16,128]{1,0:T(8,128)S(1)}, f32[16,128]{1,0:T(8,128)S(1)}, u32[]{:S(2)}, u32[]{:S(2)}) collective-permute-start(f32[16,128]{1,0:T(8,128)S(1)} %slice.4), channel_id=1, source_target_pairs={{0,1},{1,0},{2,3},{3,2},{4,5},{5,4},{6,7},{7,6},{8,9},{9,8},{10,11... | collective-permute-start | bytes 24584 | tf_op jit(solution)/shard_map/ppermute | solution.py:33
